TPU v7x, 768 devices: a whole 4x8x12 slice. The times are simulated.
768 devices in a mesh: dom: 64 (over y, z_hi, x), band: 12 (over z_lo, core).
Axes of the slice: x: 4, y: 8, z: 12 (z_hi: 2, z_lo: 6; z = z_hi * 6 + z_lo), core: 2. Of those that a mesh axis runs over, the one named last changes fastest.
Arguments:
- states: float32 [12, 884736], P('band', 'dom'), may hold values from -6 to 6
- previous: float32 [12, 884736], P('band', 'dom'), may hold values from -6 to 6
- potential: float32 [884736], P('dom'), may hold values from -1 to 1
- screening: float32 [884736], P('dom'), may hold values from 0.25 to 1
- occupation: float32 [12], P('band'), may hold values from 0.1 to 2
- cell_scale: float32 [4096], P('dom'), may hold values from 0.5 to 2
- cell_matrix: float32 [343, 343], replicated, as said below
- connectivity: int32 [343, 4096], P(None, 'dom'), may hold values from 0 to 16806, as said below
Outputs:
- filtered: float32 [12, 884736], P('band', 'dom')
- potential_field: float32 [884736], P('dom')
Inputs may be any that keep to these rules, and one draw needn't show every extreme that they name: `connectivity`: each column lists the 343 nodes of one cell as ids into its partition's extended box, in the order (k, j, i) with i fastest, each of k, j, i running over 0 to 6; the cell spans nodes 6 cz to 6 cz + 6 along z and likewise along y and x. The columns of one partition are its 64 cells in some order. `cell_matrix`: symmetric positive definite.
All inputs are finite; a program needn't handle non-finite values.
Results may differ from a plain program's by a relative error of at most 0.0001.
Values sent between devices are 32-bit elements; how exact they have to be, the bound alone decides.
A program may use at most 32 MiB of HBM per device.

v0:
```python
import jax
import jax.numpy as jnp
import numpy as np
from jax import lax
from jax.sharding import PartitionSpec as P

DEG = 6
NPC = 343
CPX = 8
CPY = 8
CPZ = 1
ITERS = 3
OX = 48
OY = 48
OZ = 6
NOWN = 13824
NEXT = 16807
CELL_DEV = 64


filter_center = 2.0
filter_halfwidth = 2.0


def shifted(array, axis, by):
    peers = lax.axis_size(axis)
    pairs = [(i, i + by) for i in range(peers) if 0 <= i + by < peers]
    return lax.ppermute(array, axis, pairs)


def layout_info():
    dom_count = lax.axis_size("dom")
    grid_side = min(4, dom_count // 4)
    grid_x = dom_count // (grid_side * grid_side)
    position = lax.axis_index("dom")
    part_x = position % grid_x
    part_y = position // grid_x % grid_side
    part_z = position // (grid_x * grid_side)
    return (grid_x, grid_side, part_x, part_y, part_z)


def plane_values(plane, offset, allowed):
    arrived = shifted(plane, "dom", offset)
    return jnp.where(allowed, arrived, jnp.zeros_like(arrived))


def plane_sums(plane, offset, allowed):
    arrived = shifted(plane, "dom", offset)
    return jnp.where(allowed, arrived, jnp.zeros_like(arrived))


def extend(values, layout):
    grid_x, grid_side, part_x, part_y, part_z = layout
    rows_count = values.shape[0]
    blocks = values.reshape(rows_count, OZ, OY, OX)
    blocks = jnp.concatenate(
        [blocks, plane_values(blocks[:, :, :, 0:1], -1, part_x < grid_x - 1)], axis=3
    )
    blocks = jnp.concatenate(
        [blocks, plane_values(blocks[:, :, 0:1, :], -grid_x, part_y < grid_side - 1)], axis=2
    )
    blocks = jnp.concatenate(
        [blocks, plane_values(blocks[:, 0:1, :, :], -grid_x * grid_side, part_z < grid_side - 1)],
        axis=1,
    )
    return blocks.reshape(rows_count, NEXT)


def fold(summed, layout):
    grid_x, grid_side, part_x, part_y, part_z = layout
    rows_count = summed.shape[0]
    blocks = summed.reshape(rows_count, OZ + 1, OY + 1, OX + 1)
    incoming = plane_sums(blocks[:, OZ:, :, :], grid_x * grid_side, part_z > 0)
    blocks = jnp.concatenate([blocks[:, 0:1] + incoming, blocks[:, 1:OZ]], axis=1)
    incoming = plane_sums(blocks[:, :, OY:, :], grid_x, part_y > 0)
    blocks = jnp.concatenate([blocks[:, :, 0:1] + incoming, blocks[:, :, 1:OY]], axis=2)
    incoming = plane_sums(blocks[:, :, :, OX:], 1, part_x > 0)
    blocks = jnp.concatenate([blocks[:, :, :, 0:1] + incoming, blocks[:, :, :, 1:OX]], axis=3)
    return blocks.reshape(rows_count, NOWN)


def node_table(cell_count):
    table = np.zeros((DEG * cell_count + 1, DEG + 1, cell_count), np.float32)
    for cell in range(cell_count):
        for local in range(DEG + 1):
            table[DEG * cell + local, local, cell] = 1.0
    return jnp.asarray(table)


def canonical_scale(connectivity, cell_scale):
    cells = np.arange(CELL_DEV)
    first_ids = DEG * (
        cells // (CPX * CPY) * (OY + 1) * (OX + 1) + cells // CPX % CPY * (OX + 1) + cells % CPX
    )
    first_ids = jnp.asarray(first_ids.astype(np.int32))
    matches = first_ids[:, None] == connectivity[0][None, :]
    return jnp.sum(
        jnp.where(matches, cell_scale[None, :], jnp.zeros_like(cell_scale)[None, :]), axis=1
    )


def to_cells(extended):
    rows_count = extended.shape[0]
    box = extended.reshape(rows_count, OZ + 1, OY + 1, OX + 1)
    high = lax.Precision.HIGHEST
    step_one = jnp.einsum("rzyx,xcs->rzycs", box, node_table(CPX), precision=high)
    step_two = jnp.einsum("rzycs,ybq->rzbqcs", step_one, node_table(CPY), precision=high)
    step_three = jnp.einsum("rzbqcs,zap->rabcpqs", step_two, node_table(CPZ), precision=high)
    return step_three.reshape(rows_count, NPC, CELL_DEV)


def from_cells(cell_terms):
    rows_count = cell_terms.shape[0]
    edge = DEG + 1
    terms = cell_terms.reshape(rows_count, edge, edge, edge, CPZ, CPY, CPX)
    high = lax.Precision.HIGHEST
    step_one = jnp.einsum("rabcpqs,xcs->rabpqx", terms, node_table(CPX), precision=high)
    step_two = jnp.einsum("rabpqx,ybq->rapyx", step_one, node_table(CPY), precision=high)
    step_three = jnp.einsum("rapyx,zap->rzyx", step_two, node_table(CPZ), precision=high)
    return step_three.reshape(rows_count, NEXT)


def cell_sum(extended, scales, matrix):
    gathered = to_cells(extended)
    cell_terms = (
        jnp.einsum("ij,kjc->kic", matrix, gathered, precision=lax.Precision.HIGHEST) * scales
    )
    return from_cells(cell_terms)


def squares(residual):
    return lax.psum(jnp.sum(residual * residual), "dom")


def per_device(
    states, previous, potential, screening, occupation, cell_scale, cell_matrix, connectivity
):
    layout = layout_info()
    scales = canonical_scale(connectivity, cell_scale)
    extended = extend(states, layout)
    applied = fold(cell_sum(extended, scales, cell_matrix), layout)
    hamiltonian = 0.5 * applied + potential[None, :] * states
    filtered = 2.0 / filter_halfwidth * (hamiltonian - filter_center * states) - previous
    partial_density = jnp.sum(occupation[:, None] * filtered * filtered, axis=0)
    total_states = states.shape[0] * lax.axis_size("band")
    density = lax.psum(partial_density, "band")
    source = density / total_states
    solution = jnp.zeros_like(source)
    residual = source
    direction = source
    norm_now = squares(residual)
    for iteration in range(ITERS):
        extended_field = extend(direction[None, :], layout)
        summed = cell_sum(extended_field, scales, cell_matrix)
        image = fold(summed, layout)[0] + screening * direction
        step_size = norm_now / lax.psum(jnp.sum(direction * image), "dom")
        solution = solution + step_size * direction
        if iteration + 1 < ITERS:
            residual = residual - step_size * image
            norm_next = squares(residual)
            direction = residual + norm_next / norm_now * direction
            norm_now = norm_next
    return (filtered, solution)


def solution(mesh):
    in_specs = (
        P("band", "dom"),
        P("band", "dom"),
        P("dom"),
        P("dom"),
        P("band"),
        P("dom"),
        P(),
        P(None, "dom"),
    )
    out_specs = (P("band", "dom"), P("dom"))
    return jax.shard_map(
        per_device, mesh=mesh, in_specs=in_specs, out_specs=out_specs, check_vma=False
    )
```

profile of v0, /device:TPU:6, one launch (start us, length us, event | category | flops | bytes accessed | tf_op | source)
XLA Modules:
  0.0 1644.4 jit_solution(9377258462197798111)
XLA Ops:
  1.8 2.7 collective-permute-start
  5.4 15.5 collective-permute-done
  22.3 18.9 %collective-permute-done.1 = f32[1,6,1,49]{3,2,1,0:T(1,128)S(1)} collective-permute-done((f32[1,6,1,49]{3,2,1,0:T(1,128)S(1)}, f32[1,6,1,49]{3,2,1,0:T(1,128)S(1)}, u32[]{:S(2)}, u32[]{:S(2)}) %collective-permute-start.1) | collective-permute-done | bytes 1208 | tf_op jit(solution)/shard_map/ppermute | solution.py:28
  43.4 4.5 collective-permute-done.2
  48.7 3.2 convolution_bitcast_fusion.3
  51.9 1.6 fusion.8
  57.5 6.3 collective-permute-start.3
  65.4 10.9 collective-permute-start.4
  77.8 1.9 collective-permute-start.5
  80.5 4.4 collective-permute-done.5
  85.9 56.9 %psum.49 = f32[13824]{0:T(1024)S(1)} all-reduce(f32[13824]{0:T(1024)S(1)} %get-tuple-element.10), channel_id=1, replica_groups=mesh['dom'=64,'band'=12] {'band'}, use_global_device_ids=true, to_apply=%region_1.2 | all-reduce | flops 13824 | bytes 110592 | tf_op jit(solution)/shard_map/psum | solution.py:146
  143.0 1.9 collective-permute-start.6
  144.9 13.5 collective-permute-done.6
  159.8 11.7 collective-permute-done.7
  173.0 9.1 collective-permute-done.8
  182.9 3.2 convolution_bitcast_fusion.2
  186.1 1.6 fusion.11
  191.6 7.7 collective-permute-start.9
  199.3 1.5 collective-permute-done.9
  200.8 8.1 collective-permute-start.10
  210.4 4.1 collective-permute-start.11
  214.7 2.8 collective-permute-done.11
  218.4 246.0 %all-reduce = (f32[]{:T(128)}, f32[]{:T(128)}) all-reduce(f32[]{:T(128)} %get-tuple-element.3, f32[]{:T(128)} %get-tuple-element.2), channel_id=1, replica_groups=mesh['dom'=64,'band'=12] {'dom'}, use_global_device_ids=true, to_apply=%region_3.4 | all-reduce | flops 2 | bytes 16 | tf_op jit(solution)/shard_map/psum | solution.py:132
  466.3 266.5 %psum.52 = f32[]{:T(128)} all-reduce(f32[]{:T(128)} %get-tuple-element.8), channel_id=1, replica_groups=mesh['dom'=64,'band'=12] {'dom'}, use_global_device_ids=true, to_apply=%region_7.8 | all-reduce | flops 1 | bytes 8 | tf_op jit(solution)/shard_map/psum | solution.py:132
  734.2 2.3 collective-permute-start.12
  736.5 13.2 collective-permute-done.12
  751.1 10.5 collective-permute-done.13
  763.2 5.1 collective-permute-done.14
  769.0 3.2 convolution_bitcast_fusion.1
  772.2 1.6 fusion.14
  777.8 10.4 collective-permute-start.15
  788.2 1.5 collective-permute-done.15
  792.5 11.0 collective-permute-start.17
  803.6 2.6 collective-permute-done.17
  807.1 246.2 %psum.53 = f32[]{:T(128)} all-reduce(f32[]{:T(128)} %multiply_reduce_fusion.2), channel_id=1, replica_groups=mesh['dom'=64,'band'=12] {'dom'}, use_global_device_ids=true, to_apply=%region_9.10 | all-reduce | flops 1 | bytes 8 | tf_op jit(solution)/shard_map/psum | solution.py:156
  1055.3 266.7 %psum.54 = f32[]{:T(128)} all-reduce(f32[]{:T(128)} %get-tuple-element.6), channel_id=1, replica_groups=mesh['dom'=64,'band'=12] {'dom'}, use_global_device_ids=true, to_apply=%region_11.12 | all-reduce | flops 1 | bytes 8 | tf_op jit(solution)/shard_map/psum | solution.py:132
  1323.4 1.9 collective-permute-start.18
  1325.3 13.6 collective-permute-done.18
  1340.3 10.5 collective-permute-done.19
  1350.9 1.5 collective-permute-start.20
  1352.4 5.1 collective-permute-done.20
  1358.3 3.2 convolution_bitcast_fusion
  1361.5 1.6 fusion.17
  1367.0 10.4 collective-permute-start.21
  1377.5 1.5 collective-permute-done.21
  1381.7 11.0 collective-permute-start.23
  1392.8 2.6 collective-permute-done.23
  1396.3 246.2 %psum.55 = f32[]{:T(128)} all-reduce(f32[]{:T(128)} %multiply_reduce_fusion), channel_id=1, replica_groups=mesh['dom'=64,'band'=12] {'dom'}, use_global_device_ids=true, to_apply=%region_13.14 | all-reduce | flops 1 | bytes 8 | tf_op jit(solution)/shard_map/psum | solution.py:156
  (155 shorter events, 47.8 us)
Async XLA Ops:
  0.6 53.5 %copy-start = (f32[343,343]{1,0:T(8,128)S(1)}, f32[343,343]{1,0:T(8,128)}, u32[]{:S(2)}) copy-start(f32[343,343]{1,0:T(8,128)} %param.39) | copy-start | bytes 1411792
  0.6 47.3 %copy-start.1 = (f32[49,7,8,1]{0,2,1,3:T(8,128)S(1)}, f32[49,7,8,1]{0,2,1,3:T(8,128)}, u32[]{:S(2)}) copy-start(f32[49,7,8,1]{0,2,1,3:T(8,128)} %constant.74) | copy-start | bytes 32932
  0.7 48.0 %copy-start.4 = (f32[49,7,8,1,1]{0,2,4,3,1:T(8,128)S(1)}, f32[49,7,8,1,1]{0,2,4,3,1:T(8,128)}, u32[]{:S(2)}) copy-start(f32[49,7,8,1,1]{0,2,4,3,1:T(8,128)} %constant.76) | copy-start | bytes 32932
  1.8 19.1 %collective-permute-start = (f32[1,6,48,1]{3,2,1,0:T(8,128)S(1)}, f32[1,6,48,1]{3,2,1,0:T(8,128)S(1)}, u32[]{:S(2)}, u32[]{:S(2)}) collective-permute-start(f32[1,6,48,1]{3,2,1,0:T(8,128)S(1)} %bitcast.251), channel_id=1, source_target_pairs={{12,0},{24,12},{36,24},{48,36},{60,48},{72,60},{84,72},{96,84},{10... | collective-permute-start | bytes 3464 | tf_op jit(solution)/shard_map/ppermute | solution.py:28
  20.9 31.0 %copy-start.7 = (f32[7,7,1,1,1]{0,1,4,3,2:T(8,128)S(1)}, f32[7,7,1,1,1]{0,1,4,3,2:T(8,128)}, u32[]{:S(2)}) copy-start(f32[7,7,1,1,1]{0,1,4,3,2:T(8,128)} %constant.75) | copy-start | bytes 592
  21.0 20.2 %collective-permute-start.1 = (f32[1,6,1,49]{3,2,1,0:T(1,128)S(1)}, f32[1,6,1,49]{3,2,1,0:T(1,128)S(1)}, u32[]{:S(2)}, u32[]{:S(2)}) collective-permute-start(f32[1,6,1,49]{3,2,1,0:T(1,128)S(1)} %pad_maximum_fusion.18), channel_id=1, source_target_pairs={{48,0},{60,12},{72,24},{84,36},{96,48},{108,60},{120,72},{132,84},... | collective-permute-start | bytes 3536 | tf_op jit(solution)/shard_map/ppermute | solution.py:28
  41.3 6.7 collective-permute-start.2
  54.1 1.3 copy-start.3
  55.5 1.5 copy-start.6
  57.5 27.7 %copy-start.5 = (f32[1,13824]{1,0:T(1,128)S(1)}, f32[1,13824]{1,0:T(1,128)}, u32[]{:S(2)}) copy-start(f32[1,13824]{1,0:T(1,128)} %param.33) | copy-start | bytes 165892
  57.5 27.7 %copy-start.8 = (f32[13824]{0:T(1024)S(1)}, f32[13824]{0:T(1024)}, u32[]{:S(2)}) copy-start(f32[13824]{0:T(1024)} %param.35) | copy-start | bytes 165892
  57.5 27.7 %copy-start.9 = (f32[1,13824]{1,0:T(1,128)S(1)}, f32[1,13824]{1,0:T(1,128)}, u32[]{:S(2)}) copy-start(f32[1,13824]{1,0:T(1,128)} %param.34) | copy-start | bytes 165892
  57.5 7.9 collective-permute-start.3
  65.4 12.2 collective-permute-start.4
  77.8 7.0 collective-permute-start.5
  143.0 15.5 collective-permute-start.6
  158.5 12.9 collective-permute-start.7
  171.5 10.6 collective-permute-start.8
  191.6 26.1 %copy-start.2 = (f32[13824]{0:T(1024)S(1)}, f32[13824]{0:T(1024)}, u32[]{:S(2)}) copy-start(f32[13824]{0:T(1024)} %param.36) | copy-start | bytes 165892
  191.6 9.2 collective-permute-start.9
  200.8 9.5 collective-permute-start.10
  210.4 7.0 collective-permute-start.11
  734.2 15.5 collective-permute-start.12
  749.8 11.8 collective-permute-start.13
  761.6 6.7 collective-permute-start.14
  777.8 11.9 collective-permute-start.15
  789.7 2.6 collective-permute-start.16
  792.5 13.7 collective-permute-start.17
  1323.4 15.5 collective-permute-start.18
  1339.0 11.8 collective-permute-start.19
  1350.9 6.7 collective-permute-start.20
  1367.0 12.0 collective-permute-start.21
  1379.0 2.6 collective-permute-start.22
  1381.7 13.7 collective-permute-start.23
where the time goes:
time: 1670 us; the launch traced here: 1640 us
  blocking collectives  1330 us (80%)
  waiting for transfers between devices  155 us (9%)
  starting transfers between devices  104 us (6%)
  matrix products  32.6 us (2%)
    psum x3, blocking collectives, squares(): return lax.psum(jnp.sum(residual * residual), 'dom')  779 us
    psum x2, blocking collectives, per_device(): step_size = norm_now / lax.psum(jnp.sum(direction * image), 'dom')  492 us
    ppermute x24, waiting for transfers between devices, shifted(): return lax.ppermute(array, axis, pairs)  155 us
    ppermute x24, starting transfers between devices, shifted(): return lax.ppermute(array, axis, pairs)  104 us
    psum x1, blocking collectives, per_device(): density = lax.psum(partial_density, 'band')  56.9 us
  transfers between devices with their start and end apart: 24, of which 24 were waited for; matrix products, arithmetic and copies ran while one was open for 0% of the time, Pallas kernels for 0%

commit v1 on v0

v1 whole, which is shorter than its diff:
```python
import jax
import jax.numpy as jnp
from jax import lax
from jax.experimental import pallas as pl
from jax.experimental.pallas import tpu as pltpu
from jax.sharding import PartitionSpec as P

MESH = pl.DeviceIdType.MESH
F32 = jnp.float32
BF16 = jnp.bfloat16
STATES = 12
ZLO = 6
FILTER_CENTER = 2.0
FILTER_SCALE = 2.0 / 2.0


HALO = (
    ("x", (1, 0, 0)),
    ("x", (1, 0, 1)),
    ("x", (1, 1, 0)),
    ("x", (1, 1, 1)),
    ("y", (0, 1, 0)),
    ("y", (0, 1, 1)),
    ("z", (0, 0, 1)),
)


def roll(x, by, axis=1):
    by = by % x.shape[axis]
    return x if by == 0 else pltpu.roll(x, by, axis)


def iotas(rows=8, lanes=128):
    row = lax.broadcasted_iota(jnp.int32, (rows, lanes), 0)
    lane = lax.broadcasted_iota(jnp.int32, (rows, lanes), 1)
    return row, lane


def split(x):
    high = x.astype(BF16)
    return high, (x - high.astype(F32)).astype(BF16)


def column_table():
    row, lane = iotas(384, 384)
    g, cx = lane >> 3, lane & 7
    j = (g * 43) >> 8
    wanted = j * 48 + cx * 6 + (g - 6 * j)
    return jnp.where((row == wanted) & (lane < 288), 1.0, 0.0).astype(BF16)


def node_rows(rows):
    row, lane = iotas(rows, 384)
    k, v = row & 7, row >> 3
    return jnp.where((lane == 49 * k + v) & (k < 7) & (v < 49), 1.0, 0.0).astype(BF16)


def to_cells(tiles, table):
    n = tiles[0].shape[0]
    row, lane = iotas(n)
    group = lane >> 3
    chunks = []
    for cy in range(8):
        first, off = 288 * cy // 128, 288 * cy % 128
        parts = []
        for m in range(3):
            one = tiles[(first + m) % 18]
            if off:
                two = tiles[(first + m + 1) % 18]
                one = jnp.where(lane < 128 - off, roll(one, -off), roll(two, -off))
            parts.append(one)
        chunks.append(jnp.concatenate(parts, axis=1))
    stacked = jnp.concatenate(chunks, axis=0)
    high, low = split(stacked)
    both = jnp.dot(jnp.concatenate([high, low], axis=0), table, preferred_element_type=F32)
    moved = both[: 8 * n] + both[8 * n :]
    skewed = [
        [roll(moved[n * cy : n * cy + n, 128 * a : 128 * a + 128], 8 * cy) for a in range(3)]
        for cy in range(8)
    ]
    out = []
    for g in range(36):
        a, b = g // 16, g % 16
        got = jnp.where(group == b, skewed[0][a], 0.0)
        for cy in range(1, 8):
            got = jnp.where(group == (b + cy) % 16, skewed[cy][a], got)
        out.append(roll(got, -8 * b))
    return out


def from_cells(tiles, table):
    row, lane = iotas(8)
    group = lane >> 3
    placed = [roll(tiles[g], 8 * (g % 16)) for g in range(36)]
    rows = []
    for cy in range(8):
        parts = []
        for a in range(3):
            count = 16 if a < 2 else 4
            got = jnp.zeros((8, 128), F32)
            for b in range(count):
                got = jnp.where(group == (b + cy) % 16, placed[16 * a + b], got)
            parts.append(roll(got, -8 * cy))
        rows.append(jnp.concatenate(parts, axis=1))
    stacked = jnp.concatenate(rows, axis=0)
    high, low = split(stacked)
    both = lax.dot_general(
        jnp.concatenate([high, low], axis=0), table, (((1,), (1,)), ((), ())), preferred_element_type=F32
    )
    moved = both[:64] + both[64:]
    out = []
    for c in range(18):
        got = jnp.zeros((8, 128), F32)
        for cy in range(8):
            start = 288 * cy - 128 * c
            lo, hi = max(start, 0), min(start + 288, 128)
            if lo >= hi:
                continue
            off = start % 128
            for m in range(3):
                begin = start + 128 * m
                one_lo, one_hi = max(begin, lo), min(begin + 128, hi)
                if one_lo >= one_hi:
                    continue
                piece = roll(moved[8 * cy : 8 * cy + 8, 128 * m : 128 * m + 128], off)
                got = jnp.where((lane >= one_lo) & (lane < one_hi), piece, got)
        out.append(got)
    return out


def pack_ghosts(field):
    row, lane = iotas()
    cx, cy = lane & 7, lane >> 3
    x_tile = jnp.zeros((8, 128), F32)
    y_tile = jnp.zeros((8, 128), F32)
    for j in range(6):
        x_tile = jnp.where((cx == j) & (cy < 8), roll(field(6 * j), j), x_tile)
    for i in range(6):
        y_tile = jnp.where(cy == i, roll(field(i), 8 * i), y_tile)
    return x_tile, y_tile


def extended(field, xs, ys, z_row, high):
    row, lane = iotas()
    cx, cy = lane & 7, lane >> 3
    hx, hy, hz = high
    x_all = jnp.where(row == 6, roll(xs[1] * (hx * hz), 6, 0), xs[0] * hx)
    xy_all = jnp.where(row == 6, roll(xs[3] * (hx * hy * hz), 6, 0), xs[2] * (hx * hy))
    y_all = jnp.where(row == 6, roll(ys[1] * (hy * hz), 6, 0), ys[0] * hy)
    out = [None] * 49
    for g in range(36):
        above = jnp.broadcast_to(z_row(g) * hz, (8, 128))
        out[7 * (g // 6) + g % 6] = jnp.where(row == 6, above, field(g))
    for j in range(6):
        out[7 * j + 6] = jnp.where(cx == 7, roll(x_all, 7 - j), roll(out[7 * j], -1))
    for i in range(6):
        out[42 + i] = jnp.where(cy == 7, roll(y_all, 56 - 8 * i), roll(out[i], -8))
    corner = jnp.where(cx == 7, roll(x_all, -1), roll(out[0], -9))
    corner = jnp.where(cy == 7, roll(y_all, 55), corner)
    out[48] = jnp.where((cx == 7) & (cy == 7), roll(xy_all, 63), corner)
    return out


def cell_terms(tiles, matrix_high, matrix_low, scale_row):
    high = tiles.astype(BF16).astype(F32)
    low = tiles - high
    _, lane = iotas(512)
    both = jnp.where(lane < 64, high, roll(low, 64)).astype(BF16)
    got = jnp.dot(matrix_high, both, preferred_element_type=F32)
    got = got + jnp.dot(matrix_low, both, preferred_element_type=F32)
    got = got + roll(got, 64)
    return got * scale_row


def local_fold(term):
    row, lane = iotas()
    cx, cy = lane & 7, lane >> 3
    upper_x = []
    for j in range(6):
        got = term(7 * j + 6)
        if j == 0:
            got = got + jnp.where(cy >= 1, roll(term(48), 8), 0.0)
        upper_x.append(got)
    x_tile = jnp.where(lane == 62, roll(term(48), -1), 0.0)
    for j in range(6):
        x_tile = jnp.where((cx == j) & (cy < 8), roll(upper_x[j], j - 7), x_tile)
    y_tile = jnp.zeros((8, 128), F32)
    for i in range(6):
        got = term(42 + i)
        if i == 0:
            got = got + jnp.where(cx >= 1, roll(term(48), 1), 0.0)
        y_tile = jnp.where(cy == i, roll(got, 8 * i - 56), y_tile)
    out = []
    for g in range(36):
        j, i = g // 6, g % 6
        got = term(7 * j + i)
        if j == 0:
            got = got + jnp.where(cy >= 1, roll(term(42 + i), 8), 0.0)
        if i == 0:
            got = got + jnp.where(cx >= 1, roll(upper_x[j], 1), 0.0)
        out.append(got)
    return out, x_tile, y_tile


def finish_fold(partial, xs, ys, z_row, low):
    row, lane = iotas()
    cx, cy = lane & 7, lane >> 3
    lx, ly, lz = low
    kept = row < 6

    def both(tile, tile_z, mask):
        return jnp.where(kept, tile * mask, 0.0) + jnp.where(row == 0, roll(tile_z * (mask * lz), 2, 0), 0.0)

    x_all = both(xs[0], xs[1], lx)
    xy_all = both(xs[2], xs[3], lx * ly)
    y_all = both(ys[0], ys[1], ly)
    out = []
    for g in range(36):
        j, i = g // 6, g % 6
        below = jnp.broadcast_to(z_row(g) * lz, (8, 128))
        got = partial(g) + jnp.where(row == 0, below, 0.0)
        if i == 0:
            got = got + jnp.where(cx == 0, roll(x_all, -j), 0.0)
        if j == 0:
            got = got + jnp.where(cy == 0, roll(y_all, -8 * i), 0.0)
        if g == 0:
            got = got + jnp.where(lane == 0, roll(xy_all, -62), 0.0)
        out.append(jnp.where(kept & (lane < 64), got, 0.0))
    return out


def kernel(
    states_ref, previous_ref, potential_ref, screening_ref, occupation_ref, scale_ref, matrix_ref, ids_ref,
    filtered_ref, field_ref,
    pad, stage, table, padded_matrix, cell_matrix, scales,
    s_f, pps_f, grid_ext, terms, part,
    sent_x, sent_y, sent_z, got_x, got_y, got_z, z_both,
    dens, dens_in, half, half_in, full_in, vec, red_out, red_in, nat, nat_in,
    halo_send, halo_recv, band_send, band_recv, red_send, red_recv,
):
    dom, band = lax.axis_index("dom"), lax.axis_index("band")
    px, py, pz = lax.rem(dom, 4), lax.rem(lax.div(dom, 4), 4), lax.div(dom, 16)
    z_lo, core = lax.div(band, 2), lax.rem(band, 2)
    z_hi = lax.rem(py, 2)

    def place(x, y, z):
        return x + 4 * y + 16 * z

    def near(step, sign, mirrored):
        x = lax.rem(px + (sign * step[0] + 4), 4)
        y = lax.rem(py + (sign * step[1] + 4), 4)
        z = lax.rem(pz + (sign * step[2] + 4), 4)
        flipped = mirrored and step[1] % 2 == 1
        return (place(x, y, z), 2 * (ZLO - 1 - z_lo) + core if flipped else band)

    partner = (dom, 2 * z_lo + (1 - core))

    def chip(z):
        return (dom, 2 * z + core)

    group_one, group_two = [], []
    for e in range(1, 8):
        x = lax.rem(px + e % 4, 4)
        y = lax.rem(py + 2 * (e // 4), 4)
        group_one.append((place(x, y, pz), band))
    for e in range(1, 8):
        z = lax.rem(pz + e % 4, 4)
        if e // 4:
            y = py + 1 - 2 * z_hi
            group_two.append((place(px, y, z), 2 * (ZLO - 1 - z_lo) + core))
        else:
            group_two.append((place(px, py, z), band))

    greeted = []
    for _, step in HALO:
        for sign in (1, -1):
            greeted.append(near(step, sign, False))
            if step[1]:
                greeted.append(near(step, sign, True))
    greeted.append(partner)
    for e in range(1, ZLO):
        greeted.append(chip(lax.rem(z_lo + e, ZLO)))
    greeted += group_one + group_two
    barrier = pltpu.get_barrier_semaphore()
    for device in greeted:
        pl.semaphore_signal(barrier, inc=1, device_id=device, device_id_type=MESH)

    def flag(test):
        return jnp.where(test, 1.0, 0.0).astype(F32)

    high = (flag(px < 3), flag(py < 3), flag(pz < 3))
    low = (flag(px > 0), flag(py > 0), flag(pz > 0))
    row, lane = iotas()

    table[...] = column_table()
    pad[...] = jnp.zeros_like(pad)
    sent_z[...] = jnp.zeros_like(sent_z)
    pad[0, 0:108, :] = states_ref[...]
    first = to_cells([pad[0, pl.ds(c, 8, stride=18), :] for c in range(18)], table[...])
    for g in range(36):
        s_f[8 * g : 8 * g + 8, :] = first[g]
    grid_ext[...] = jnp.zeros_like(grid_ext)

    def copies(at, mirrored, sign):
        made = []
        counts = {"x": 0, "y": 0, "z": 0}
        for e, (kind, step) in enumerate(HALO):
            c = counts[kind]
            counts[kind] += 1
            src = {"x": sent_x, "y": sent_y, "z": sent_z}[kind].at[at]
            dst = {"x": got_x.at[at, c], "y": got_y.at[at, c], "z": got_z.at[at]}[kind]
            made.append(
                pltpu.make_async_remote_copy(
                    src_ref=src,
                    dst_ref=dst,
                    send_sem=halo_send.at[at, e],
                    recv_sem=halo_recv.at[at, e],
                    device_id=near(step, sign, mirrored),
                    device_id_type=MESH,
                )
            )
        return made

    def put_z(at, source, sublane):
        lower = source[pl.ds(sublane, 18, stride=8), :]
        upper = source[pl.ds(144 + sublane, 18, stride=8), :]
        _, wide = iotas(18)
        sent_z[at, 0:18, :] = jnp.where(wide < 64, lower, roll(upper, 64))

    def take_z(at):
        rows = got_z[at]
        z_both[0] = rows
        z_both[1] = roll(rows, 64)

    def z_row(g):
        return z_both[g // 18, g % 18 : g % 18 + 1, :]

    def start_extend(n, source, mirrored):
        at = 2 * n
        x_tile, y_tile = pack_ghosts(lambda g: source[8 * g : 8 * g + 8, :])
        sent_x[at] = x_tile
        sent_y[at] = y_tile
        put_z(at, source, 0)
        made = copies(at, mirrored, -1)
        for copy in made:
            copy.start()
        return made

    def middle(n, source, made, mirrored):
        at = 2 * n
        for copy in made:
            copy.wait_recv()
        take_z(at)
        tiles = extended(
            lambda g: source[8 * g : 8 * g + 8, :],
            [got_x[at, c] for c in range(4)],
            [got_y[at, c] for c in range(2)],
            z_row,
            high,
        )
        for v in range(49):
            grid_ext[8 * v : 8 * v + 8, :] = tiles[v]
        terms[...] = cell_terms(grid_ext[...], cell_matrix[0], cell_matrix[1], scales[0:1, :])
        folded, x_tile, y_tile = local_fold(lambda v: terms[8 * v : 8 * v + 8, :])
        sent_x[at + 1] = x_tile
        sent_y[at + 1] = y_tile
        for g in range(36):
            part[8 * g : 8 * g + 8, :] = folded[g]
        put_z(at + 1, part, 6)
        out = copies(at + 1, mirrored, 1)
        for copy in out:
            copy.start()
        return out

    def finish(n, made):
        at = 2 * n + 1
        for copy in made:
            copy.wait_recv()
        take_z(at)
        return finish_fold(
            lambda g: part[8 * g : 8 * g + 8, :],
            [got_x[at, c] for c in range(4)],
            [got_y[at, c] for c in range(2)],
            z_row,
            low,
        )

    pl.semaphore_wait(barrier, len(greeted))
    extend_0 = start_extend(0, s_f, False)

    pad[1, 0:108, :] = previous_ref[...]
    pad[2, 0:108, :] = potential_ref[...]
    pad[3, 0:108, :] = screening_ref[...]
    three = to_cells(
        [
            jnp.concatenate([pad[m, pl.ds(c, 8, stride=18), :] for m in (1, 2, 3)], axis=0)
            for c in range(18)
        ],
        table[...],
    )
    for g in range(36):
        for m in range(3):
            pps_f[m, 8 * g : 8 * g + 8, :] = three[g][8 * m : 8 * m + 8]
    padded_matrix[...] = jnp.zeros_like(padded_matrix)
    padded_matrix[0:343, 0:343] = matrix_ref[...]
    by_row, by_column = node_rows(400), node_rows(512)
    for h, piece in enumerate(split(padded_matrix[...])):
        rows_moved = jnp.dot(by_row, piece, preferred_element_type=F32).astype(BF16)
        cell_matrix[h] = lax.dot_general(
            rows_moved, by_column, (((1,), (1,)), ((), ())), preferred_element_type=F32
        ).astype(BF16)
    own_row, _ = iotas(128, 64)
    first_id = 6 * 49 * ((own_row & 63) >> 3) + 6 * (own_row & 7)
    matches = jnp.where(first_id == ids_ref[0:1, :], 1.0, 0.0).astype(F32)
    given = jnp.broadcast_to(scale_ref[...], (8, 64))
    scales[...] = lax.dot_general(
        given, matches, (((1,), (1,)), ((), ())), precision=lax.Precision.HIGHEST, preferred_element_type=F32
    )

    fold_0 = middle(0, s_f, extend_0, False)
    summed = finish(0, fold_0)
    weight = occupation_ref[...]
    kept = []
    squares = []
    for g in range(36):
        rows = slice(8 * g, 8 * g + 8)
        here = s_f[rows, :]
        hamiltonian = 0.5 * summed[g] + pps_f[1, rows, :] * here
        value = FILTER_SCALE * (hamiltonian - FILTER_CENTER * here) - pps_f[0, rows, :]
        stage[rows, :] = value
        squares.append(weight * value * value)
    for m in range(18):
        dens[8 * m : 8 * m + 8, :] = squares[m] + roll(squares[m + 18], 64)

    mine = pl.multiple_of(72 * core, 8)
    other = pl.multiple_of(72 * (1 - core), 8)

    def band_copy(src, dst, at_send, at_recv, device):
        return pltpu.make_async_remote_copy(
            src_ref=src,
            dst_ref=dst,
            send_sem=band_send.at[at_send],
            recv_sem=band_recv.at[at_recv],
            device_id=device,
            device_id_type=MESH,
        )

    swap = band_copy(dens.at[pl.ds(other, 72), :], dens_in, 0, 0, partner)
    swap.start()
    swap.wait_recv()
    half[...] = dens[pl.ds(mine, 72), :] + dens_in[...]

    not_first, not_last = z_lo > 0, z_lo < ZLO - 1
    slot_first = jnp.maximum(z_lo - 1, 0)
    slot_last = jnp.minimum(z_lo, ZLO - 2)

    to_first = band_copy(half, half_in.at[slot_first], 1, 1 + slot_first, chip(0))
    to_last = band_copy(half, half_in.at[slot_last], 2, 1 + slot_last, chip(ZLO - 1))

    @pl.when(not_first)
    def _():
        to_first.start()

    @pl.when(not_last)
    def _():
        to_last.start()

    natural = from_cells([stage[8 * g : 8 * g + 8, :] for g in range(36)], table[...])
    for c in range(18):
        nat[0, pl.ds(c, 8, stride=18), :] = natural[c]
    filtered_ref[...] = nat[0, 0:108, :]

    is_end = (z_lo == 0) | (z_lo == ZLO - 1)

    @pl.when(is_end)
    def _():
        arrived = [band_copy(half, half_in.at[s], 1, 1 + s, partner) for s in range(ZLO - 1)]
        for copy in arrived:
            copy.wait_recv()
        total = half[...]
        for s in range(ZLO - 1):
            total = total + half_in[s]
        dens_own = total * (1.0 / STATES)
        full_in[0] = dens_own
        again = band_copy(full_in.at[0], full_in.at[1], 3, 6, partner)
        again.start()
        again.wait_recv()
        first_half = jnp.where(core == 0, full_in[0], full_in[1])
        second_half = jnp.where(core == 0, full_in[1], full_in[0])
        both = (first_half, second_half)
        R, W, Q, SS, PP = 0, 1, 2, 3, 4
        for m in range(18):
            tile = both[m // 9][8 * (m % 9) : 8 * (m % 9) + 8]
            vec[R, 8 * m : 8 * m + 8, :] = jnp.where(lane < 64, tile, 0.0)
            vec[R, 8 * (m + 18) : 8 * (m + 18) + 8, :] = jnp.where(lane < 64, roll(tile, 64), 0.0)

        def with_screening(got, v):
            return [
                got[g] + pps_f[2, 8 * g : 8 * g + 8, :] * vec[v, 8 * g : 8 * g + 8, :] for g in range(36)
            ]

        def put(v, tiles):
            for g in range(36):
                vec[v, 8 * g : 8 * g + 8, :] = tiles[g]

        def dot_row(a, b):
            got = vec[a] * vec[b]
            return jnp.sum(got, axis=0, keepdims=True)

        def start_reduce(n, pairs):
            tile = jnp.zeros((8, 128), F32)
            for m, (a, b) in enumerate(pairs):
                tile = jnp.where(row == m, jnp.broadcast_to(dot_row(a, b), (8, 128)), tile)
            red_out[n, 0] = tile
            return send_reduce(n, 0, group_one)

        def send_reduce(n, level, devices):
            made = []
            for e, device in enumerate(devices):
                made.append(
                    pltpu.make_async_remote_copy(
                        src_ref=red_out.at[n, level],
                        dst_ref=red_in.at[n, level, e],
                        send_sem=red_send.at[n, level, e],
                        recv_sem=red_recv.at[n, level, e],
                        device_id=device,
                        device_id_type=MESH,
                    )
                )
            for copy in made:
                copy.start()
            return made

        def take(n, level, made):
            for copy in made:
                copy.wait_recv()
            got = red_out[n, level]
            for e in range(7):
                got = got + red_in[n, level, e]
            return got

        def second_level(n, made):
            red_out[n, 1] = take(n, 0, made)
            return send_reduce(n, 1, group_two)

        def scalars(n, made):
            got = jnp.sum(take(n, 1, made), axis=1, keepdims=True)
            return got[0:1], got[1:2], got[2:3]

        everything = []

        made = start_extend(1, vec.at[R], True)
        out = middle(1, vec.at[R], made, True)
        put(W, with_screening(finish(1, out), R))
        everything += made + out

        red_a = start_reduce(0, ((R, R), (R, W)))
        made = start_extend(2, vec.at[W], True)
        red_b = second_level(0, red_a)
        out = middle(2, vec.at[W], made, True)
        put(Q, with_screening(finish(2, out), W))
        norm_0, image_0, _ = scalars(0, red_b)
        everything += made + out + red_a + red_b

        alpha_0 = norm_0 / image_0
        vec[PP] = vec[R]
        vec[SS] = vec[W]
        vec[5] = alpha_0 * vec[R]
        vec[6] = vec[Q]
        vec[R] = vec[R] - alpha_0 * vec[SS]
        vec[W] = vec[W] - alpha_0 * vec[Q]

        red_a = start_reduce(1, ((R, R), (R, W), (R, SS)))
        made = start_extend(3, vec.at[W], True)
        red_b = second_level(1, red_a)
        out = middle(3, vec.at[W], made, True)
        put(Q, with_screening(finish(3, out), W))
        norm_1, rw_1, rs_1 = scalars(1, red_b)
        everything += made + out + red_a + red_b

        beta_1 = norm_1 / norm_0
        image_1 = rw_1 + 2.0 * beta_1 * rs_1 + beta_1 * beta_1 * image_0
        alpha_1 = norm_1 / image_1
        vec[PP] = vec[R] + beta_1 * vec[PP]
        vec[SS] = vec[W] + beta_1 * vec[SS]
        vec[6] = vec[Q] + beta_1 * vec[6]
        vec[5] = vec[5] + alpha_1 * vec[PP]
        vec[R] = vec[R] - alpha_1 * vec[SS]
        vec[W] = vec[W] - alpha_1 * vec[6]

        red_a = start_reduce(2, ((R, R), (R, W), (R, SS)))
        red_b = second_level(2, red_a)
        norm_2, rw_2, rs_2 = scalars(2, red_b)
        everything += red_a + red_b
        beta_2 = norm_2 / norm_1
        image_2 = rw_2 + 2.0 * beta_2 * rs_2 + beta_2 * beta_2 * image_1
        alpha_2 = norm_2 / image_2
        vec[5] = vec[5] + alpha_2 * (vec[R] + beta_2 * vec[PP])

        natural = from_cells([vec[5, 8 * g : 8 * g + 8, :] for g in range(36)], table[...])
        for c in range(18):
            nat[1, pl.ds(c, 8, stride=18), :] = natural[c]
        onward = [
            band_copy(nat.at[1, 0:112], nat_in, 4 + s, 7, chip(jnp.where(z_lo == 0, 1 + s, ZLO - 2 - s)))
            for s in range(2)
        ]
        for copy in onward:
            copy.start()
        field_ref[...] = nat[1, 0:108, :]
        again.wait_send()
        for copy in everything + onward:
            copy.wait_send()

    @pl.when(jnp.logical_not(is_end))
    def _():
        band_copy(nat.at[1, 0:112], nat_in, 4, 7, partner).wait_recv()
        field_ref[...] = nat_in[0:108, :]

    swap.wait_send()

    @pl.when(not_first)
    def _():
        to_first.wait_send()

    @pl.when(not_last)
    def _():
        to_last.wait_send()

    for copy in extend_0 + fold_0:
        copy.wait_send()


def per_device(states, previous, potential, screening, occupation, cell_scale, cell_matrix, connectivity):
    vmem = pl.BlockSpec(memory_space=pltpu.VMEM)
    filtered, field = pl.pallas_call(
        kernel,
        out_shape=(jax.ShapeDtypeStruct((108, 128), F32), jax.ShapeDtypeStruct((108, 128), F32)),
        in_specs=[vmem] * 8,
        out_specs=(vmem, vmem),
        scratch_shapes=[
            pltpu.VMEM((4, 144, 128), F32),
            pltpu.VMEM((288, 128), F32),
            pltpu.VMEM((384, 384), BF16),
            pltpu.VMEM((384, 384), F32),
            pltpu.VMEM((2, 400, 512), BF16),
            pltpu.VMEM((8, 128), F32),
            pltpu.VMEM((288, 128), F32),
            pltpu.VMEM((3, 288, 128), F32),
            pltpu.VMEM((512, 128), F32),
            pltpu.VMEM((400, 128), F32),
            pltpu.VMEM((288, 128), F32),
            pltpu.VMEM((8, 8, 128), F32),
            pltpu.VMEM((8, 8, 128), F32),
            pltpu.VMEM((8, 24, 128), F32),
            pltpu.VMEM((8, 4, 8, 128), F32),
            pltpu.VMEM((8, 2, 8, 128), F32),
            pltpu.VMEM((8, 24, 128), F32),
            pltpu.VMEM((2, 24, 128), F32),
            pltpu.VMEM((144, 128), F32),
            pltpu.VMEM((72, 128), F32),
            pltpu.VMEM((72, 128), F32),
            pltpu.VMEM((5, 72, 128), F32),
            pltpu.VMEM((2, 72, 128), F32),
            pltpu.VMEM((7, 288, 128), F32),
            pltpu.VMEM((3, 2, 8, 128), F32),
            pltpu.VMEM((3, 2, 7, 8, 128), F32),
            pltpu.VMEM((2, 144, 128), F32),
            pltpu.VMEM((112, 128), F32),
            pltpu.SemaphoreType.DMA((8, 7)),
            pltpu.SemaphoreType.DMA((8, 7)),
            pltpu.SemaphoreType.DMA((6,)),
            pltpu.SemaphoreType.DMA((8,)),
            pltpu.SemaphoreType.DMA((3, 2, 7)),
            pltpu.SemaphoreType.DMA((3, 2, 7)),
        ],
        compiler_params=pltpu.CompilerParams(collective_id=0, has_side_effects=True),
        name="step",
    )(
        states.reshape(108, 128),
        previous.reshape(108, 128),
        potential.reshape(108, 128),
        screening.reshape(108, 128),
        occupation.reshape(1, 1),
        cell_scale.reshape(1, 64),
        cell_matrix,
        connectivity[0:1, :],
    )
    return filtered.reshape(1, 13824), field.reshape(13824)


def solution(mesh):
    in_specs = (
        P("band", "dom"),
        P("band", "dom"),
        P("dom"),
        P("dom"),
        P("band"),
        P("dom"),
        P(),
        P(None, "dom"),
    )
    out_specs = (P("band", "dom"), P("dom"))
    return jax.shard_map(per_device, mesh=mesh, in_specs=in_specs, out_specs=out_specs, check_vma=False)
```

time: 1670 us -> 109 us (0.07); the launches traced: 1640 us -> 109 us
  blocking collectives: 1330 us -> 0 us
  waiting for transfers between devices: 155 us -> 0 us
  starting transfers between devices: 104 us -> 0 us
  Pallas kernels: 0 us -> 103 us
  matrix products: 32.6 us -> 0 us
    psum x6 -> x0, blocking collectives: 1330 us -> none  [the longest x3 779 us: squares(): return lax.psum(jnp.sum(residual * residual), 'dom')]
    ppermute x24 -> x0, waiting for transfers between devices: 155 us -> none  [shifted(): return lax.ppermute(array, axis, pairs)]
    ppermute x24 -> x0, starting transfers between devices: 104 us -> none  [shifted(): return lax.ppermute(array, axis, pairs)]
    pallas_call x0 -> x1, Pallas kernels: none -> 103 us  [per_device(): pl.pallas_call(kernel, out_shape=(jax.ShapeDtypeStruct((108, 128), F32),...]
    dot_general x28 -> x0, matrix products: 32.6 us -> none  [the longest x4 12.8 us: to_cells(): jnp.einsum('rzycs,ybq->rzbqcs', step_one, node_table(CPY), precision=high)]
  transfers between devices with their start and end apart: 24 -> 0, of which waited for: 24 -> 0; matrix products, arithmetic and copies ran while one was open for 0% -> 0% of each run, Pallas kernels for 0% -> 0%
where the time goes in v1:
time: 109 us
  Pallas kernels  103 us (94%)
  local copies, waits for them, and re-layouts  3.56 us (3%)
  other arithmetic  1.5 us (1%)
  between operations  1.31 us (1%)
    pallas_call x1, Pallas kernels, per_device(): pl.pallas_call(kernel, out_shape=(jax.ShapeDtypeStruct((108, 128), F32),...  103 us
    unnamed x9, local copies, waits for them, and re-layouts  2.81 us

profile of v1, /device:TPU:6, one launch (start us, length us, event | category | flops | bytes accessed | tf_op | source)
XLA Modules:
  0.0 108.9 jit_solution(4660503195998065091)
XLA Ops:
  1.3 0.0 slice-start
  1.3 0.0 copy-start.1
  1.3 0.7 slice-done
  2.0 0.6 copy.11.ids_ref
  2.6 0.0 copy-done.1
  2.6 0.0 copy-start.2
  2.6 0.8 reduce
  3.4 0.1 copy-done.2
  3.5 0.7 reduce.1
  4.2 102.6 %step.1 = (f32[108,128]{1,0:T(8,128)}, f32[108,128]{1,0:T(8,128)}) custom-call(f32[108,128]{1,0:T(8,128)} %bitcast.13, f32[108,128]{1,0:T(8,128)} %bitcast.14, f32[108,128]{1,0:T(8,128)} %bitcast.17, f32[108,128]{1,0:T(8,128)} %bitcast.18, f32[1,1]{1,0:T(1,128)} %bitcast.12.occupation_ref, f32[1,64]{1,0:T(1,128)} %bitcast.20, f32[343,343]{1,0:T(8,128)} %matrix_ref.1, ...), custom_call_target="tpu_custom_call" | custom-call | tf_op jit(solution)/shard_map/step/pallas_call | solution.py:635
  106.8 0.0 copy-start
  106.8 1.5 %copy.14 = f32[1,1,108,128]{3,1,2,0:T(1,128)} copy(f32[1,1,108,128]{3,2,1,0:T(8,128)} %bitcast.16) | data formatting | bytes 110592
  108.3 0.0 copy-done
  108.3 0.6 copy.17
Async XLA Ops:
  1.3 0.8 slice-start
  1.3 1.4 %copy-start.1 = (f32[1,13824]{1,0:T(1,128)S(1)}, f32[1,13824]{1,0:T(1,128)}, u32[]{:S(2)}) copy-start(f32[1,13824]{1,0:T(1,128)} %param.8) | copy-start | bytes 165892
  2.6 0.8 copy-start.2
  106.8 1.5 %copy-start = (f32[108,128]{1,0:T(8,128)S(1)}, f32[108,128]{1,0:T(8,128)}, u32[]{:S(2)}) copy-start(f32[108,128]{1,0:T(8,128)} %get-tuple-element.5) | copy-start | bytes 165892

commit v2 on v1

v2 whole, which is shorter than its diff:
```python
import jax
import jax.numpy as jnp
from jax import lax
from jax.experimental import pallas as pl
from jax.experimental.pallas import tpu as pltpu
from jax.sharding import PartitionSpec as P

MESH = pl.DeviceIdType.MESH
F32 = jnp.float32
BF16 = jnp.bfloat16
STATES = 12
ZLO = 6
FILTER_CENTER = 2.0
FILTER_SCALE = 2.0 / 2.0


AROUND = [(x, y, z) for y in (1, -1, 0) for x in (1, -1, 0) for z in (1, -1, 0) if (x, y, z) != (0, 0, 0)]
BELOW = [d for d in AROUND if max(d) <= 0]
TILES = 38
CORE_ROWS = 288
ROWS = 8 * TILES


def side(step):
    return 0 if step > 0 else 1

def roll(x, by, axis=1):
    by = by % x.shape[axis]
    return x if by == 0 else pltpu.roll(x, by, axis)


def iotas(rows=8, lanes=128):
    row = lax.broadcasted_iota(jnp.int32, (rows, lanes), 0)
    lane = lax.broadcasted_iota(jnp.int32, (rows, lanes), 1)
    return row, lane


def split(x):
    high = x.astype(BF16)
    return high, (x - high.astype(F32)).astype(BF16)


def column_table():
    row, lane = iotas(384, 384)
    g, cx = lane >> 3, lane & 7
    j = (g * 43) >> 8
    wanted = j * 48 + cx * 6 + (g - 6 * j)
    return jnp.where((row == wanted) & (lane < 288), 1.0, 0.0).astype(BF16)


def node_rows(rows):
    row, lane = iotas(rows, 384)
    k, v = row & 7, row >> 3
    return jnp.where((lane == 49 * k + v) & (k < 7) & (v < 49), 1.0, 0.0).astype(BF16)


def to_cells(tiles, table):
    n = tiles[0].shape[0]
    row, lane = iotas(n)
    group = lane >> 3
    chunks = []
    for cy in range(8):
        first, off = 288 * cy // 128, 288 * cy % 128
        parts = []
        for m in range(3):
            one = tiles[(first + m) % 18]
            if off:
                two = tiles[(first + m + 1) % 18]
                one = jnp.where(lane < 128 - off, roll(one, -off), roll(two, -off))
            parts.append(one)
        chunks.append(jnp.concatenate(parts, axis=1))
    stacked = jnp.concatenate(chunks, axis=0)
    high, low = split(stacked)
    both = jnp.dot(jnp.concatenate([high, low], axis=0), table, preferred_element_type=F32)
    moved = both[: 8 * n] + both[8 * n :]
    skewed = [
        [roll(moved[n * cy : n * cy + n, 128 * a : 128 * a + 128], 8 * cy) for a in range(3)]
        for cy in range(8)
    ]
    out = []
    for g in range(36):
        a, b = g // 16, g % 16
        got = jnp.where(group == b, skewed[0][a], 0.0)
        for cy in range(1, 8):
            got = jnp.where(group == (b + cy) % 16, skewed[cy][a], got)
        out.append(roll(got, -8 * b))
    return out


def split_exact(x):
    high, low = split(x)
    return high, low, (x - high.astype(F32) - low.astype(F32)).astype(BF16)


def from_cells(tiles, table):
    row, lane = iotas(8)
    group = lane >> 3
    placed = [roll(tiles[g], 8 * (g % 16)) for g in range(36)]
    rows = []
    for cy in range(8):
        parts = []
        for a in range(3):
            count = 16 if a < 2 else 4
            got = jnp.zeros((8, 128), F32)
            for b in range(count):
                got = jnp.where(group == (b + cy) % 16, placed[16 * a + b], got)
            parts.append(roll(got, -8 * cy))
        rows.append(jnp.concatenate(parts, axis=1))
    stacked = jnp.concatenate(rows, axis=0)
    both = lax.dot_general(
        jnp.concatenate(split_exact(stacked), axis=0), table, (((1,), (1,)), ((), ())), preferred_element_type=F32
    )
    moved = both[:64] + both[64:128] + both[128:]
    out = []
    for c in range(18):
        got = jnp.zeros((8, 128), F32)
        for cy in range(8):
            start = 288 * cy - 128 * c
            lo, hi = max(start, 0), min(start + 288, 128)
            if lo >= hi:
                continue
            off = start % 128
            for m in range(3):
                begin = start + 128 * m
                one_lo, one_hi = max(begin, lo), min(begin + 128, hi)
                if one_lo >= one_hi:
                    continue
                piece = roll(moved[8 * cy : 8 * cy + 8, 128 * m : 128 * m + 128], off)
                got = jnp.where((lane >= one_lo) & (lane < one_hi), piece, got)
        out.append(got)
    return out


def cell_terms(tiles, matrix_high, matrix_low, scale_row):
    high = tiles.astype(BF16).astype(F32)
    low = tiles - high
    _, lane = iotas(512)
    both = jnp.where(lane < 64, high, roll(low, 64)).astype(BF16)
    got = jnp.dot(matrix_high, both, preferred_element_type=F32)
    got = got + jnp.dot(matrix_low, both, preferred_element_type=F32)
    got = got + roll(got, 64)
    return got * scale_row


def local_fold(term):
    row, lane = iotas()
    cx, cy = lane & 7, lane >> 3
    upper_x = []
    for j in range(6):
        got = term(7 * j + 6)
        if j == 0:
            got = got + jnp.where(cy >= 1, roll(term(48), 8), 0.0)
        upper_x.append(got)
    x_tile = jnp.where(lane == 62, roll(term(48), -1), 0.0)
    for j in range(6):
        x_tile = jnp.where((cx == j) & (cy < 8), roll(upper_x[j], j - 7), x_tile)
    y_tile = jnp.zeros((8, 128), F32)
    for i in range(6):
        got = term(42 + i)
        if i == 0:
            got = got + jnp.where(cx >= 1, roll(term(48), 1), 0.0)
        y_tile = jnp.where(cy == i, roll(got, 8 * i - 56), y_tile)
    out = []
    for g in range(36):
        j, i = g // 6, g % 6
        got = term(7 * j + i)
        if j == 0:
            got = got + jnp.where(cy >= 1, roll(term(42 + i), 8), 0.0)
        if i == 0:
            got = got + jnp.where(cx >= 1, roll(upper_x[j], 1), 0.0)
        out.append(got)
    return out, x_tile, y_tile


def column_to_row(tile, at):
    row, lane = iotas()
    return jnp.sum(jnp.where(row == lane, jnp.broadcast_to(tile[:, at : at + 1], (8, 128)), 0.0), axis=0, keepdims=True)


def row_to_column(values):
    row, lane = iotas()
    return jnp.sum(jnp.where(row == lane, jnp.broadcast_to(values, (8, 128)), 0.0), axis=1, keepdims=True)


def wide(values):
    return jnp.broadcast_to(values, (8, 128))


def low_faces(field):
    row, lane = iotas()
    cx, cy = lane & 7, lane >> 3
    x_tile = jnp.zeros((8, 128), F32)
    y_tile = jnp.zeros((8, 128), F32)
    for j in range(6):
        x_tile = jnp.where((cx == j) & (cy < 8), roll(field(6 * j), j), x_tile)
    for i in range(6):
        y_tile = jnp.where(cy == i, roll(field(i), 8 * i), y_tile)
    return x_tile, y_tile


def from_above(field, x_tile, x_row, y_tile, y_row, edge, corner, z_row, high):
    row, lane = iotas()
    hx, hy, hz = high
    line = jnp.where(lane[0:1] == 6, roll(corner * hz, 6), edge)
    x_all = jnp.where(row == 6, wide(x_row * hz), x_tile)
    x_all = hx * jnp.where(lane == 62, wide(row_to_column(line) * hy), x_all)
    y_all = hy * jnp.where(row == 6, wide(y_row * hz), y_tile)
    core = [jnp.where(row == 6, wide(z_row(g) * hz), field(g)) for g in range(36)]
    return core + [x_all, y_all]


def extended(field):
    row, lane = iotas()
    cx, cy = lane & 7, lane >> 3
    x_all, y_all = field(36), field(37)
    out = [None] * 49
    for g in range(36):
        out[7 * (g // 6) + g % 6] = field(g)
    for j in range(6):
        out[7 * j + 6] = jnp.where(cx == 7, roll(x_all, 7 - j), roll(field(6 * j), -1))
    for i in range(6):
        out[42 + i] = jnp.where(cy == 7, roll(y_all, 56 - 8 * i), roll(field(i), -8))
    corner = jnp.where(cx == 7, roll(x_all, -1), roll(field(0), -9))
    corner = jnp.where(cy == 7, roll(y_all, 55), corner)
    out[48] = jnp.where(lane == 63, roll(x_all, 1), corner)
    return out


def shared(part, x_high, y_high):
    row, lane = iotas()
    x_low, y_low = low_faces(part)
    x_low = jnp.where(lane == 62, roll(y_high, 62), x_low)
    y_out = jnp.where(lane == 55, roll(x_high, -7), y_high)
    y_low = jnp.where(lane == 55, roll(x_high, 55), y_low)
    edges = [column_to_row(t, at) for t in (x_high, x_low) for at in (62, 0)]
    return (x_high, x_low), (y_out, y_low), edges


def absorb(part, x_high, y_high, xs, x_rows, ys, y_rows, edges, z_row, low, high):
    row, lane = iotas()
    cx, cy = lane & 7, lane >> 3
    hx, hy, hz = high
    lx, ly, lz = low

    def with_rows(tile, rows):
        return tile + jnp.where(row == 6, wide(rows[0]), jnp.where(row == 0, wide(rows[1] * lz), 0.0))

    x_up, x_down = with_rows(xs[0], x_rows[0]), with_rows(xs[1], x_rows[1]) * lx
    y_up, y_down = with_rows(ys[0], y_rows[0]), with_rows(ys[1], y_rows[1]) * ly
    lines = edges[0] + jnp.where(lane == 6, roll(edges[1], 6), jnp.where(lane == 0, roll(edges[2] * lz, -6), 0.0))
    columns = [wide(row_to_column(lines[c : c + 1])) for c in range(4)]
    up_row, down_row = row == 6, row == 0

    def vertical(up, down):
        return jnp.where(up_row, wide(up), jnp.where(down_row, wide(down * lz), 0.0))

    x_all = x_high + x_up + vertical(z_row(0, 36), z_row(1, 36))
    x_all = x_all + jnp.where(lane == 62, roll(y_up, 7) + columns[0], 0.0)
    x_all = x_all + jnp.where(lane == 0, roll(y_down, -55) + columns[1] * ly, 0.0)
    y_all = y_high + jnp.where(cy < 6, y_up, 0.0) + vertical(z_row(0, 37), z_row(1, 37))
    y_all = y_all + jnp.where(lane == 0, roll(x_down, -62) + columns[2] * lx, 0.0)
    top = jnp.where(up_row, hz, 1.0)
    x_all = x_all * (top * hx) * jnp.where(lane == 62, hy, 1.0)
    y_all = y_all * (top * hy)
    inside = jnp.where(lane < 64, top, 0.0)
    out = []
    for g in range(36):
        j, i = g // 6, g % 6
        got = part(g) + vertical(z_row(0, g), z_row(1, g))
        if i == 0:
            got = got + jnp.where((cx == 0) & (cy < 8), roll(x_down, -j), 0.0)
        if j == 0:
            got = got + jnp.where(cy == 0, roll(y_down, -8 * i), 0.0)
        if g == 0:
            got = got + jnp.where(lane == 0, columns[3] * (lx * ly), 0.0)
        out.append(jnp.where(lane < 64, got * inside, 0.0))
    return out + [x_all, y_all]


def kernel(
    states_ref, previous_ref, potential_ref, screening_ref, occupation_ref, scale_ref, matrix_ref, ids_ref,
    filtered_ref, field_ref,
    pad, raw_matrix, ids, table, padded_matrix, cell_matrix, scales,
    own, screen, vec, grid_ext, terms, part, faces,
    sent_x, sent_y, sent_z, sent_e, got_x, got_y, got_z, got_xr, got_yr, got_e, z_both,
    dens, dens_in, half, half_in, full_in, red_out, red_in, nat, nat_f, factors,
    in_sem, out_sem, halo_send, halo_recv, band_send, band_recv, red_send, red_recv,
):
    dom, band = lax.axis_index("dom"), lax.axis_index("band")
    px, py, pz = lax.rem(dom, 4), lax.rem(lax.div(dom, 4), 4), lax.div(dom, 16)
    z_lo, core = lax.div(band, 2), lax.rem(band, 2)
    z_hi = lax.rem(py, 2)
    across = 2 * (ZLO - 1 - z_lo) + core

    def place(x, y, z):
        return x + 4 * y + 16 * z

    def near(step, mirrored):
        x = lax.rem(px + (step[0] + 4), 4)
        y = lax.rem(py + (step[1] + 4), 4)
        z = lax.rem(pz + (step[2] + 4), 4)
        return (place(x, y, z), across if mirrored and step[1] else band)

    partner = (dom, 2 * z_lo + (1 - core))

    def chip(z):
        return (dom, 2 * z + core)

    group_one = [(place(lax.rem(px + e % 4, 4), lax.rem(py + 2 * (e // 4), 4), pz), band) for e in range(1, 8)]
    group_two = []
    for e in range(1, 8):
        z = lax.rem(pz + e % 4, 4)
        if e // 4:
            group_two.append((place(px, py + 1 - 2 * z_hi, z), across))
        else:
            group_two.append((place(px, py, z), band))

    greeted = [near(step, False) for step in AROUND]
    greeted += [near(step, True) for step in AROUND if step[1]]
    greeted.append(partner)
    greeted += [chip(lax.rem(z_lo + e, ZLO)) for e in range(1, ZLO)]
    greeted += group_one + group_two
    barrier = pltpu.get_barrier_semaphore()
    for device in greeted:
        pl.semaphore_signal(barrier, inc=1, device_id=device, device_id_type=MESH)

    loads = [
        pltpu.make_async_copy(states_ref.at[:, 0, :], pad.at[0, pl.ds(0, 108), :], in_sem.at[0]),
        pltpu.make_async_copy(previous_ref.at[:, 0, :], pad.at[1, pl.ds(0, 108), :], in_sem.at[1]),
        pltpu.make_async_copy(potential_ref, pad.at[2, pl.ds(0, 108), :], in_sem.at[2]),
        pltpu.make_async_copy(screening_ref, pad.at[3, pl.ds(0, 108), :], in_sem.at[3]),
        pltpu.make_async_copy(matrix_ref, raw_matrix, in_sem.at[4]),
        pltpu.make_async_copy(ids_ref.at[:, pl.ds(0, 128)], ids, in_sem.at[5]),
    ]
    for load in loads:
        load.start()

    def flag(test):
        return jnp.where(test, 1.0, 0.0).astype(F32)

    high = (flag(px < 3), flag(py < 3), flag(pz < 3))
    low = (flag(px > 0), flag(py > 0), flag(pz > 0))
    row, lane = iotas()

    table[...] = column_table()
    for m in range(4):
        pad[m, 108:144, :] = jnp.zeros((36, 128), F32)
    grid_ext[...] = jnp.zeros_like(grid_ext)
    sent_z[...] = jnp.zeros_like(sent_z)
    loads[0].wait()
    first = to_cells([pad[0, pl.ds(c, 8, stride=18), :] for c in range(18)], table[...])
    for g in range(36):
        own[8 * g : 8 * g + 8, :] = first[g]

    def tile_of(source):
        return lambda g: source[8 * g : 8 * g + 8, :]

    def copy_to(at, step, mirrored):
        x, y, z = step
        s, t = side(-x), side(-y)
        if x and y:
            src = sent_e.at[at, pl.ds(2 * side(x) + side(y), 1)]
            dst = got_e.at[at, 0 if z == 0 else 1 + side(-z), pl.ds(2 * s + t, 1)]
        elif x:
            src, dst = sent_x.at[at, side(x)], got_x.at[at, s]
            if z:
                src = src.at[pl.ds(6 if z > 0 else 0, 1)]
                dst = got_xr.at[at, pl.ds(2 * s + side(-z), 1)]
        elif y:
            src, dst = sent_y.at[at, side(y)], got_y.at[at, t]
            if z:
                src = src.at[pl.ds(6 if z > 0 else 0, 1)]
                dst = got_yr.at[at, pl.ds(2 * t + side(-z), 1)]
        else:
            src, dst = sent_z.at[at, side(z)], got_z.at[at, side(-z)]
        e = AROUND.index(step)
        return pltpu.make_async_remote_copy(
            src_ref=src,
            dst_ref=dst,
            send_sem=halo_send.at[at, e],
            recv_sem=halo_recv.at[at, e],
            device_id=near(step, mirrored),
            device_id_type=MESH,
        )

    def start_copies(at, steps, mirrored):
        made = [copy_to(at, step, mirrored) for step in steps]
        for copy in made:
            copy.start()
        return made

    _, lane_18 = iotas(18)

    def put_z(at, s, source, sublane):
        lower = source[pl.ds(sublane, 18, stride=8), :]
        upper = source[pl.ds(144 + sublane, 18, stride=8), :]
        sent_z[at, s, 0:18, :] = jnp.where(lane_18 < 64, lower, roll(upper, 64))

    def take_z(at, s):
        rows = got_z[at, s]
        z_both[s, 0] = rows
        z_both[s, 1] = roll(rows, 64)

    def z_row(s, m):
        if m >= 36:
            return z_both[s, 0, m - 18 : m - 17, :]
        return z_both[s, m // 18, m % 18 : m % 18 + 1, :]

    def products(source):
        tiles = extended(tile_of(source))
        for v in range(49):
            grid_ext[8 * v : 8 * v + 8, :] = tiles[v]
        terms[...] = cell_terms(grid_ext[...], cell_matrix[0], cell_matrix[1], scales[0:1, :])

    def start_sums(at, source, factor, extra, mirrored):
        products(source)
        folded, x_high, y_high = local_fold(lambda v: terms[8 * v : 8 * v + 8, :])
        for g in range(36):
            part[8 * g : 8 * g + 8, :] = factor * folded[g] + extra(g)
        x_high, y_high = factor * x_high, factor * y_high
        faces[0], faces[1] = x_high, y_high
        xs, ys, edges = shared(tile_of(part), x_high, y_high)
        for s in range(2):
            sent_x[at, s] = xs[s]
            sent_y[at, s] = ys[s]
            put_z(at, s, part, 6 if s == 0 else 0)
            k = 6 if s == 0 else 0
            sent_z[at, s, 18:19, :] = x_high[k : k + 1]
            sent_z[at, s, 19:20, :] = y_high[k : k + 1]
        for c in range(4):
            sent_e[at, c : c + 1, :] = edges[c]
        return start_copies(at, AROUND, mirrored)

    def finish_sums(at, made):
        for copy in made:
            copy.wait_recv()
        take_z(at, 0)
        take_z(at, 1)
        return absorb(
            tile_of(part),
            faces[0],
            faces[1],
            [got_x[at, s] for s in range(2)],
            [[got_xr[at, 2 * s + t : 2 * s + t + 1, :] for t in range(2)] for s in range(2)],
            [got_y[at, s] for s in range(2)],
            [[got_yr[at, 2 * s + t : 2 * s + t + 1, :] for t in range(2)] for s in range(2)],
            [got_e[at, t] for t in range(3)],
            z_row,
            low,
            high,
        )

    x_tile, y_tile = low_faces(tile_of(own))
    sent_x[0, 1] = x_tile
    sent_y[0, 1] = y_tile
    sent_e[0, 3:4, :] = column_to_row(own[0:8, :], 0)
    put_z(0, 1, own, 0)
    pl.semaphore_wait(barrier, len(greeted))
    ghosts = start_copies(0, BELOW, False)

    for load in loads[1:]:
        load.wait()
    three = to_cells(
        [
            jnp.concatenate([pad[m, pl.ds(c, 8, stride=18), :] for m in (1, 2, 3)], axis=0)
            for c in range(18)
        ],
        table[...],
    )
    for g in range(36):
        rows = slice(8 * g, 8 * g + 8)
        screen[rows, :] = three[g][16:24]
        vec[0, rows, :] = FILTER_SCALE * ((three[g][8:16] - FILTER_CENTER) * own[rows, :]) - three[g][0:8]
    padded_matrix[...] = jnp.zeros_like(padded_matrix)
    padded_matrix[0:343, 0:343] = raw_matrix[...]
    by_row, by_column = node_rows(400), node_rows(512)
    for h, piece in enumerate(split(padded_matrix[...])):
        rows_moved = jnp.dot(by_row, piece, preferred_element_type=F32).astype(BF16)
        cell_matrix[h] = lax.dot_general(
            rows_moved, by_column, (((1,), (1,)), ((), ())), preferred_element_type=F32
        ).astype(BF16)
    _, lane_64 = iotas(64)
    first_id = 6 * 49 * ((lane_64 & 63) >> 3) + 6 * (lane_64 & 7)
    matches = jnp.where(first_id == jnp.broadcast_to(ids[:, 0:1], (64, 128)), 1.0, 0.0).astype(F32)
    given = jnp.broadcast_to(scale_ref[...], (8, 64))
    scales[...] = jnp.dot(given, matches, precision=lax.Precision.HIGHEST, preferred_element_type=F32)

    for copy in ghosts:
        copy.wait_recv()
    take_z(0, 0)
    compact = from_above(
        tile_of(own),
        got_x[0, 0],
        got_xr[0, 0:1, :],
        got_y[0, 0],
        got_yr[0, 0:1, :],
        got_e[0, 0, 0:1, :],
        got_e[0, 1, 0:1, :],
        lambda g: z_row(0, g),
        high,
    )
    for m in range(TILES):
        vec[1, 8 * m : 8 * m + 8, :] = compact[m]
    summing = start_sums(1, vec.at[1], 0.5 * FILTER_SCALE, tile_of(vec.at[0]), False)
    values = finish_sums(1, summing)
    weight = occupation_ref[0]
    squares = [weight * value * value for value in values]
    for m in range(20):
        tile = squares[m]
        if m + 20 < TILES:
            tile = tile + roll(squares[m + 20], 64)
        dens[8 * m : 8 * m + 8, :] = tile

    mine = pl.multiple_of(80 * core, 8)
    other = pl.multiple_of(80 * (1 - core), 8)

    def band_copy(src, dst, at_send, at_recv, device):
        return pltpu.make_async_remote_copy(
            src_ref=src,
            dst_ref=dst,
            send_sem=band_send.at[at_send],
            recv_sem=band_recv.at[at_recv],
            device_id=device,
            device_id_type=MESH,
        )

    swap = band_copy(dens.at[pl.ds(other, 80), :], dens_in, 0, 0, partner)
    swap.start()
    for m in range(36):
        vec[0, 8 * m : 8 * m + 8, :] = values[m]
    swap.wait_recv()
    half[...] = dens[pl.ds(mine, 80), :] + dens_in[...]

    not_first, not_last = z_lo > 0, z_lo < ZLO - 1
    slot_first = jnp.maximum(z_lo - 1, 0)
    slot_last = jnp.minimum(z_lo, ZLO - 2)
    to_first = band_copy(half, half_in.at[slot_first], 1, 1 + slot_first, chip(0))
    to_last = band_copy(half, half_in.at[slot_last], 2, 1 + slot_last, chip(ZLO - 1))

    @pl.when(not_first)
    def _():
        to_first.start()

    @pl.when(not_last)
    def _():
        to_last.start()

    natural = from_cells([jnp.where(row < 6, vec[0, 8 * g : 8 * g + 8, :], 0.0) for g in range(36)], table[...])
    for c in range(18):
        nat_f[pl.ds(c, 8, stride=18), :] = natural[c]
    store = pltpu.make_async_copy(nat_f.at[pl.ds(0, 108), :], filtered_ref.at[:, 0, :], out_sem)
    store.start()

    is_end = (z_lo == 0) | (z_lo == ZLO - 1)
    B, W, Q, R1, W1 = 0, 1, 2, 3, 4

    @pl.when(is_end)
    def _():
        arrived = [band_copy(half, half_in.at[s], 1, 1 + s, partner) for s in range(ZLO - 1)]
        for copy in arrived:
            copy.wait_recv()
        total = half[...]
        for s in range(ZLO - 1):
            total = total + half_in[s]
        full_in[0] = total * (1.0 / STATES)
        again = band_copy(full_in.at[0], full_in.at[1], 3, 6, partner)
        again.start()
        again.wait_recv()
        both = (
            jnp.where(core == 0, full_in[0], full_in[1]),
            jnp.where(core == 0, full_in[1], full_in[0]),
        )
        for m in range(20):
            tile = both[m // 10][8 * (m % 10) : 8 * (m % 10) + 8]
            vec[B, 8 * m : 8 * m + 8, :] = jnp.where(lane < 64, tile, 0.0)
            if m + 20 < TILES:
                vec[B, 8 * (m + 20) : 8 * (m + 20) + 8, :] = jnp.where(lane < 64, roll(tile, 64), 0.0)

        def put(v, tiles):
            for m in range(TILES):
                vec[v, 8 * m : 8 * m + 8, :] = tiles[m]

        def screened(v):
            return lambda g: screen[8 * g : 8 * g + 8, :] * vec[v, 8 * g : 8 * g + 8, :]

        def onto_row(got):
            got = jnp.sum(got.reshape(36, 8, 128), axis=0)
            return jnp.sum(jnp.where(row < 6, got, 0.0), axis=0, keepdims=True)

        def dot_row(a, b):
            return onto_row(vec[a, 0:CORE_ROWS, :] * vec[b, 0:CORE_ROWS, :])

        def send_reduce(n, level, devices):
            made = [
                pltpu.make_async_remote_copy(
                    src_ref=red_out.at[n, level],
                    dst_ref=red_in.at[n, level, e],
                    send_sem=red_send.at[n, level, e],
                    recv_sem=red_recv.at[n, level, e],
                    device_id=device,
                    device_id_type=MESH,
                )
                for e, device in enumerate(devices)
            ]
            for copy in made:
                copy.start()
            return made

        def start_reduce(n, rows):
            tile = jnp.zeros((8, 128), F32)
            for m, values in enumerate(rows):
                tile = jnp.where(row == m, wide(values), tile)
            red_out[n, 0] = tile
            return send_reduce(n, 0, group_one)

        def take(n, level, made):
            for copy in made:
                copy.wait_recv()
            got = red_out[n, level]
            for e in range(7):
                got = got + red_in[n, level, e]
            return got

        def second_level(n, made):
            red_out[n, 1] = take(n, 0, made)
            return send_reduce(n, 1, group_two)

        def scalars(n, made, count):
            got = jnp.sum(take(n, 1, made), axis=1, keepdims=True)
            return [got[m : m + 1] for m in range(count)]

        def hand_on(n, v):
            natural = from_cells(
                [jnp.where(row < 6, vec[v, 8 * g : 8 * g + 8, :], 0.0) for g in range(36)], table[...]
            )
            for c in range(18):
                nat[n, pl.ds(c, 8, stride=18), :] = natural[c]
            return onward(nat.at[n, 0:112], nat.at[n, 0:112], n)

        def onward(src, dst, n):
            made = [
                band_copy(src, dst, 4 + 2 * n + s, 7 + n, chip(jnp.where(z_lo == 0, 1 + s, ZLO - 2 - s)))
                for s in range(2)
            ]
            for copy in made:
                copy.start()
            return made

        sent = [again]
        made = start_sums(2, vec.at[B], 1.0, screened(B), True)
        sent += made + hand_on(0, B)
        put(W, finish_sums(2, made))

        red_a = start_reduce(0, [dot_row(B, B), dot_row(B, W)])
        made = start_sums(3, vec.at[W], 1.0, screened(W), True)
        red_b = second_level(0, red_a)
        sent += made + red_a + red_b + hand_on(1, W)
        put(Q, finish_sums(3, made))
        norm_0, image_0 = scalars(0, red_b, 2)
        alpha_0 = norm_0 / image_0

        vec[R1] = vec[B] - alpha_0 * vec[W]
        vec[W1] = vec[W] - alpha_0 * vec[Q]
        products(vec.at[W1])
        energy = jnp.sum((grid_ext[0:392, :] * terms[0:392, :]).reshape(49, 8, 128), axis=0)
        energy = jnp.sum(jnp.where(lane < 64, energy, 0.0), axis=0, keepdims=True)
        owned = vec[W1, 0:CORE_ROWS, :]
        energy = energy + onto_row(screen[...] * owned * owned)
        red_a = start_reduce(
            1,
            [
                dot_row(R1, R1),
                dot_row(R1, W1),
                dot_row(R1, W),
                dot_row(W1, W1),
                dot_row(W1, W),
                energy,
                dot_row(W1, Q),
                dot_row(W, Q),
            ],
        )
        sent += hand_on(2, Q)
        red_b = second_level(1, red_a)
        norm_1, rw, rv, ww, wv, waw, wav, vav = scalars(1, red_b, 8)
        c_b, c_w, c_q = combine(alpha_0, norm_0, image_0, norm_1, rw, rv, ww, wv, waw, wav, vav)
        tile = jnp.where(row == 0, wide(c_b), jnp.where(row == 1, wide(c_w), wide(c_q)))
        factors[0] = tile
        sent += red_a + red_b + onward(factors.at[0], factors.at[1], 3)
        field_ref[...] = c_b * nat[0, 0:108, :] + c_w * nat[1, 0:108, :] + c_q * nat[2, 0:108, :]
        for copy in sent:
            copy.wait_send()

    @pl.when(jnp.logical_not(is_end))
    def _():
        for n in range(3):
            band_copy(nat.at[n, 0:112], nat.at[n, 0:112], 4, 7 + n, partner).wait_recv()
        band_copy(factors.at[0], factors.at[1], 4, 10, partner).wait_recv()
        field_ref[...] = (
            factors[1, 0:1, :] * nat[0, 0:108, :]
            + factors[1, 1:2, :] * nat[1, 0:108, :]
            + factors[1, 2:3, :] * nat[2, 0:108, :]
        )

    swap.wait_send()

    @pl.when(not_first)
    def _():
        to_first.wait_send()

    @pl.when(not_last)
    def _():
        to_last.wait_send()

    for copy in ghosts + summing:
        copy.wait_send()
    store.wait()


def combine(alpha_0, norm_0, image_0, norm_1, rw, rv, ww, wv, waw, wav, vav):
    beta_1 = norm_1 / norm_0
    image_1 = rw + 2.0 * beta_1 * rv + beta_1 * beta_1 * image_0
    alpha_1 = norm_1 / image_1
    r_s = rw + beta_1 * rv
    s_s = ww + 2.0 * beta_1 * wv + beta_1 * beta_1 * (wv_self(alpha_0, wv, vav))
    r_as = ww + beta_1 * wv
    s_as = waw + 2.0 * beta_1 * wav + beta_1 * beta_1 * vav
    norm_2 = jnp.maximum(norm_1 - 2.0 * alpha_1 * r_s + alpha_1 * alpha_1 * s_s, 0.0)
    r2_ar2 = rw - 2.0 * alpha_1 * r_as + alpha_1 * alpha_1 * s_as
    r2_s = r_s - alpha_1 * s_s
    beta_2 = norm_2 / norm_1
    image_2 = r2_ar2 + 2.0 * beta_2 * r2_s + beta_2 * beta_2 * image_1
    alpha_2 = jnp.where(image_2 > 0.0, norm_2 / image_2, 0.0)
    grown = alpha_0 + alpha_1 * (1.0 + beta_1)
    c_b = grown + alpha_2 * (1.0 + beta_2 * (1.0 + beta_1))
    c_w = -alpha_1 * alpha_0 - alpha_2 * (grown + beta_2 * alpha_0)
    c_q = alpha_2 * alpha_1 * alpha_0
    return c_b, c_w, c_q


def wv_self(alpha_0, wv, vav):
    return wv + alpha_0 * vav


def per_device(states, previous, potential, screening, occupation, cell_scale, cell_matrix, connectivity):
    vmem = pl.BlockSpec(memory_space=pltpu.VMEM)
    anywhere = pl.BlockSpec(memory_space=pl.ANY)
    scalar = pl.BlockSpec(memory_space=pltpu.SMEM)
    filtered, field = pl.pallas_call(
        kernel,
        out_shape=(jax.ShapeDtypeStruct((108, 1, 128), F32), jax.ShapeDtypeStruct((108, 128), F32)),
        in_specs=[anywhere] * 4 + [scalar, vmem, anywhere, anywhere],
        out_specs=(anywhere, vmem),
        scratch_shapes=[
            pltpu.VMEM((4, 144, 128), F32),
            pltpu.VMEM((343, 343), F32),
            pltpu.VMEM((64, 128), jnp.int32),
            pltpu.VMEM((384, 384), BF16),
            pltpu.VMEM((384, 384), F32),
            pltpu.VMEM((2, 400, 512), BF16),
            pltpu.VMEM((8, 128), F32),
            pltpu.VMEM((288, 128), F32),
            pltpu.VMEM((288, 128), F32),
            pltpu.VMEM((5, ROWS, 128), F32),
            pltpu.VMEM((512, 128), F32),
            pltpu.VMEM((400, 128), F32),
            pltpu.VMEM((288, 128), F32),
            pltpu.VMEM((2, 8, 128), F32),
            pltpu.VMEM((4, 2, 8, 128), F32),
            pltpu.VMEM((4, 2, 8, 128), F32),
            pltpu.VMEM((4, 2, 24, 128), F32),
            pltpu.VMEM((4, 8, 128), F32),
            pltpu.VMEM((4, 2, 8, 128), F32),
            pltpu.VMEM((4, 2, 8, 128), F32),
            pltpu.VMEM((4, 2, 24, 128), F32),
            pltpu.VMEM((4, 8, 128), F32),
            pltpu.VMEM((4, 8, 128), F32),
            pltpu.VMEM((4, 3, 8, 128), F32),
            pltpu.VMEM((2, 2, 24, 128), F32),
            pltpu.VMEM((160, 128), F32),
            pltpu.VMEM((80, 128), F32),
            pltpu.VMEM((80, 128), F32),
            pltpu.VMEM((5, 80, 128), F32),
            pltpu.VMEM((2, 80, 128), F32),
            pltpu.VMEM((2, 2, 8, 128), F32),
            pltpu.VMEM((2, 2, 7, 8, 128), F32),
            pltpu.VMEM((3, 144, 128), F32),
            pltpu.VMEM((144, 128), F32),
            pltpu.VMEM((2, 8, 128), F32),
            pltpu.SemaphoreType.DMA((6,)),
            pltpu.SemaphoreType.DMA,
            pltpu.SemaphoreType.DMA((4, 26)),
            pltpu.SemaphoreType.DMA((4, 26)),
            pltpu.SemaphoreType.DMA((12,)),
            pltpu.SemaphoreType.DMA((11,)),
            pltpu.SemaphoreType.DMA((2, 2, 7)),
            pltpu.SemaphoreType.DMA((2, 2, 7)),
        ],
        compiler_params=pltpu.CompilerParams(collective_id=0, has_side_effects=True),
        name="step",
    )(
        states.reshape(108, 1, 128),
        previous.reshape(108, 1, 128),
        potential.reshape(108, 128),
        screening.reshape(108, 128),
        occupation,
        cell_scale.reshape(1, 64),
        cell_matrix,
        connectivity.T,
    )
    return filtered.reshape(1, 13824), field.reshape(13824)


def solution(mesh):
    in_specs = (
        P("band", "dom"),
        P("band", "dom"),
        P("dom"),
        P("dom"),
        P("band"),
        P("dom"),
        P(),
        P(None, "dom"),
    )
    out_specs = (P("band", "dom"), P("dom"))
    return jax.shard_map(per_device, mesh=mesh, in_specs=in_specs, out_specs=out_specs, check_vma=False)
```

time: 109 us -> 81.7 us (0.75)
  Pallas kernels: 103 us -> 77.4 us
  other arithmetic: 1.5 us -> 0 us
  local copies, waits for them, and re-layouts: 3.56 us -> 2.09 us
    pallas_call x1, Pallas kernels: 103 us -> 77.4 us  [per_device(): pl.pallas_call(kernel, out_shape=(jax.ShapeDtypeStruct((108, 1, 128), F32...]
    unnamed x2 -> x0, other arithmetic: 1.5 us -> none
    unnamed x9 -> x4, local copies, waits for them, and re-layouts: 2.81 us -> 2.09 us
where the time goes in v2:
time: 81.7 us; the launch traced here: 80.8 us
  Pallas kernels  77.4 us (95%)
  local copies, waits for them, and re-layouts  2.09 us (3%)
  between operations  1.29 us (2%)
    pallas_call x1, Pallas kernels, per_device(): pl.pallas_call(kernel, out_shape=(jax.ShapeDtypeStruct((108, 1, 128), F32...  77.4 us
    unnamed x4, local copies, waits for them, and re-layouts  2.09 us

profile of v2, /device:TPU:6, one launch (start us, length us, event | category | flops | bytes accessed | tf_op | source)
XLA Modules:
  0.0 80.8 jit_solution(6971702471131175959)
XLA Ops:
  1.3 77.4 %step.1 = (f32[108,1,128]{2,1,0:T(1,128)}, f32[108,128]{1,0:T(8,128)}) custom-call(f32[108,1,128]{2,1,0:T(1,128)} %bitcast.13, f32[108,1,128]{2,1,0:T(1,128)} %bitcast.14, f32[108,128]{1,0:T(8,128)} %bitcast.10, f32[108,128]{1,0:T(8,128)} %bitcast.11, f32[1]{0:T(128)S(6)} %copy.12.occupation_ref, f32[1,64]{1,0:T(1,128)} %bitcast.15, f32[343,343]{1,0:T(8,128)} %matrix_ref.1, ...), custom_call_target="tpu_custom_call" | custom-call | tf_op jit(solution)/shard_map/step/pallas_call | solution.py:748
  78.7 0.0 copy-start
  78.7 1.5 %copy.13 = f32[1,13824]{1,0:T(1,128)} copy(f32[1,13824]{1,0:T(1,128)} %bitcast.12) | data formatting | bytes 110592
  80.2 0.0 copy-done
  80.2 0.6 copy.14
Async XLA Ops:
  78.7 1.5 %copy-start = (f32[108,128]{1,0:T(8,128)S(1)}, f32[108,128]{1,0:T(8,128)}, u32[]{:S(2)}) copy-start(f32[108,128]{1,0:T(8,128)} %get-tuple-element.5) | copy-start | bytes 165892

commit v3 on v2

--- a/solution.py
+++ b/solution.py
@@ -15,7 +15,8 @@
 
 
 AROUND = [(x, y, z) for y in (1, -1, 0) for x in (1, -1, 0) for z in (1, -1, 0) if (x, y, z) != (0, 0, 0)]
-BELOW = [d for d in AROUND if max(d) <= 0]
+LEVEL = [d for d in AROUND if d[1] == 0]
+BELOW = [d for d in LEVEL if max(d) <= 0]
 TILES = 38
 CORE_ROWS = 288
 ROWS = 8 * TILES
@@ -198,13 +199,11 @@
     return x_tile, y_tile
 
 
-def from_above(field, x_tile, x_row, y_tile, y_row, edge, corner, z_row, high):
-    row, lane = iotas()
-    hx, hy, hz = high
-    line = jnp.where(lane[0:1] == 6, roll(corner * hz, 6), edge)
-    x_all = jnp.where(row == 6, wide(x_row * hz), x_tile)
-    x_all = hx * jnp.where(lane == 62, wide(row_to_column(line) * hy), x_all)
-    y_all = hy * jnp.where(row == 6, wide(y_row * hz), y_tile)
+def from_above(field, x_tile, x_row, y_all, y_row, z_row, high):
+    row, _ = iotas()
+    hx, _, hz = high
+    x_all = hx * jnp.where(row == 6, wide(x_row * hz), x_tile)
+    y_all = jnp.where(row == 6, wide(y_row * hz), y_all)
     core = [jnp.where(row == 6, wide(z_row(g) * hz), field(g)) for g in range(36)]
     return core + [x_all, y_all]
 
@@ -234,6 +233,41 @@
     y_low = jnp.where(lane == 55, roll(x_high, 55), y_low)
     edges = [column_to_row(t, at) for t in (x_high, x_low) for at in (62, 0)]
     return (x_high, x_low), (y_out, y_low), edges
+
+
+def with_y(part, x_high, y_high, y_up, y_down):
+    row, lane = iotas()
+    cy = lane >> 3
+    first = [part(i) + jnp.where(cy == 0, roll(y_down, -8 * i), 0.0) for i in range(6)]
+    x_high = x_high + jnp.where(lane == 62, roll(y_up, 7), jnp.where(lane == 0, roll(y_down, -55), 0.0))
+    return first, x_high, y_high + jnp.where(cy < 6, y_up, 0.0)
+
+
+def absorb_level(part, x_high, y_high, xs, x_rows, z_row, low, high):
+    row, lane = iotas()
+    cx, cy = lane & 7, lane >> 3
+    hx, hy, hz = high
+    lx, _, lz = low
+    up_row, down_row = row == 6, row == 0
+
+    def vertical(up, down):
+        return jnp.where(up_row, wide(up), jnp.where(down_row, wide(down * lz), 0.0))
+
+    x_up = xs[0] + vertical(x_rows[0][0], x_rows[0][1])
+    x_down = (xs[1] + vertical(x_rows[1][0], x_rows[1][1])) * lx
+    x_all = x_high + x_up + vertical(z_row(0, 36), z_row(1, 36))
+    y_all = y_high + vertical(z_row(0, 37), z_row(1, 37))
+    y_all = y_all + jnp.where(lane == 0, roll(x_down, -62), 0.0)
+    top = jnp.where(up_row, hz, 1.0)
+    x_all = x_all * (top * hx) * jnp.where(lane == 62, hy, 1.0)
+    y_all = y_all * (top * hy)
+    out = []
+    for g in range(36):
+        got = part(g) + vertical(z_row(0, g), z_row(1, g))
+        if g % 6 == 0:
+            got = got + jnp.where((cx == 0) & (cy < 8), roll(x_down, -(g // 6)), 0.0)
+        out.append(jnp.where(lane < 64, got * top, 0.0))
+    return out + [x_all, y_all]
 
 
 def absorb(part, x_high, y_high, xs, x_rows, ys, y_rows, edges, z_row, low, high):
@@ -306,23 +340,31 @@
     def chip(z):
         return (dom, 2 * z + core)
 
-    group_one = [(place(lax.rem(px + e % 4, 4), lax.rem(py + 2 * (e // 4), 4), pz), band) for e in range(1, 8)]
-    group_two = []
+    y_at = lax.div(dom, 8)
+    group_one, group_two = [], []
     for e in range(1, 8):
-        z = lax.rem(pz + e % 4, 4)
-        if e // 4:
-            group_two.append((place(px, py + 1 - 2 * z_hi, z), across))
-        else:
-            group_two.append((place(px, py, z), band))
-
-    greeted = [near(step, False) for step in AROUND]
-    greeted += [near(step, True) for step in AROUND if step[1]]
+        x = lax.rem(px + e % 4, 4)
+        y = py + 1 - 2 * z_hi if e // 4 else py
+        group_one.append((place(x, y, pz), across if e // 4 else band))
+    for e in range(1, 8):
+        group_two.append((lax.rem(dom, 8) + 8 * lax.rem(y_at + e, 8), band))
+
+    is_end = (z_lo == 0) | (z_lo == ZLO - 1)
+    greeted = [near((0, 1, 0), False), near((0, -1, 0), False)] + [near(step, False) for step in LEVEL]
     greeted.append(partner)
     greeted += [chip(lax.rem(z_lo + e, ZLO)) for e in range(1, ZLO)]
-    greeted += group_one + group_two
+    ends_greeted = [near(step, True) for step in AROUND if step[1]] + group_one + group_two
     barrier = pltpu.get_barrier_semaphore()
-    for device in greeted:
-        pl.semaphore_signal(barrier, inc=1, device_id=device, device_id_type=MESH)
+
+    def greet(devices):
+        for device in devices:
+            pl.semaphore_signal(barrier, inc=1, device_id=device, device_id_type=MESH)
+
+    greet(greeted)
+
+    @pl.when(is_end)
+    def _():
+        greet(ends_greeted)
 
     loads = [
         pltpu.make_async_copy(states_ref.at[:, 0, :], pad.at[0, pl.ds(0, 108), :], in_sem.at[0]),
@@ -412,21 +454,28 @@
             grid_ext[8 * v : 8 * v + 8, :] = tiles[v]
         terms[...] = cell_terms(grid_ext[...], cell_matrix[0], cell_matrix[1], scales[0:1, :])
 
-    def start_sums(at, source, factor, extra, mirrored):
+    def cell_sums(source, factor, extra):
         products(source)
         folded, x_high, y_high = local_fold(lambda v: terms[8 * v : 8 * v + 8, :])
         for g in range(36):
             part[8 * g : 8 * g + 8, :] = factor * folded[g] + extra(g)
-        x_high, y_high = factor * x_high, factor * y_high
-        faces[0], faces[1] = x_high, y_high
-        xs, ys, edges = shared(tile_of(part), x_high, y_high)
+        faces[0], faces[1] = factor * x_high, factor * y_high
+
+    def put_level(at, xs, x_high, y_high):
         for s in range(2):
+            k = 6 if s == 0 else 0
             sent_x[at, s] = xs[s]
-            sent_y[at, s] = ys[s]
-            put_z(at, s, part, 6 if s == 0 else 0)
-            k = 6 if s == 0 else 0
+            put_z(at, s, part, k)
             sent_z[at, s, 18:19, :] = x_high[k : k + 1]
             sent_z[at, s, 19:20, :] = y_high[k : k + 1]
+
+    def start_sums(at, source, factor, extra, mirrored):
+        cell_sums(source, factor, extra)
+        x_high, y_high = faces[0], faces[1]
+        xs, ys, edges = shared(tile_of(part), x_high, y_high)
+        put_level(at, xs, x_high, y_high)
+        for s in range(2):
+            sent_y[at, s] = ys[s]
         for c in range(4):
             sent_e[at, c : c + 1, :] = edges[c]
         return start_copies(at, AROUND, mirrored)
@@ -451,12 +500,18 @@
         )
 
     x_tile, y_tile = low_faces(tile_of(own))
-    sent_x[0, 1] = x_tile
     sent_y[0, 1] = y_tile
-    sent_e[0, 3:4, :] = column_to_row(own[0:8, :], 0)
     put_z(0, 1, own, 0)
-    pl.semaphore_wait(barrier, len(greeted))
-    ghosts = start_copies(0, BELOW, False)
+
+    @pl.when(is_end)
+    def _():
+        pl.semaphore_wait(barrier, len(greeted) + len(ends_greeted))
+
+    @pl.when(jnp.logical_not(is_end))
+    def _():
+        pl.semaphore_wait(barrier, len(greeted))
+
+    ghosts = start_copies(0, [(0, -1, 0)], False)
 
     for load in loads[1:]:
         load.wait()
@@ -485,24 +540,48 @@
     given = jnp.broadcast_to(scale_ref[...], (8, 64))
     scales[...] = jnp.dot(given, matches, precision=lax.Precision.HIGHEST, preferred_element_type=F32)
 
-    for copy in ghosts:
+    ghosts[0].wait_recv()
+    y_all = got_y[0, 0] * high[1]
+    sent_x[0, 1] = jnp.where(lane == 62, roll(y_all, 62), x_tile)
+    sent_z[0, 1, 19:20, :] = y_all[0:1]
+    ghosts_level = start_copies(0, BELOW, False)
+    for copy in ghosts_level:
         copy.wait_recv()
     take_z(0, 0)
     compact = from_above(
-        tile_of(own),
-        got_x[0, 0],
-        got_xr[0, 0:1, :],
-        got_y[0, 0],
-        got_yr[0, 0:1, :],
-        got_e[0, 0, 0:1, :],
-        got_e[0, 1, 0:1, :],
-        lambda g: z_row(0, g),
-        high,
+        tile_of(own), got_x[0, 0], got_xr[0, 0:1, :], y_all, z_row(0, 37), lambda g: z_row(0, g), high
     )
     for m in range(TILES):
         vec[1, 8 * m : 8 * m + 8, :] = compact[m]
-    summing = start_sums(1, vec.at[1], 0.5 * FILTER_SCALE, tile_of(vec.at[0]), False)
-    values = finish_sums(1, summing)
+
+    cell_sums(vec.at[1], 0.5 * FILTER_SCALE, tile_of(vec.at[0]))
+    x_high, y_high = faces[0], faces[1]
+    _, ys, _ = shared(tile_of(part), x_high, y_high)
+    for s in range(2):
+        sent_y[1, s] = ys[s]
+    summing = start_copies(1, [(0, 1, 0), (0, -1, 0)], False)
+    for copy in summing:
+        copy.wait_recv()
+    along, x_high, y_high = with_y(tile_of(part), x_high, y_high, got_y[1, 0], got_y[1, 1] * low[1])
+    for i in range(6):
+        part[8 * i : 8 * i + 8, :] = along[i]
+    xs, _, _ = shared(tile_of(part), x_high, y_high)
+    put_level(1, xs, x_high, y_high)
+    summing_level = start_copies(1, LEVEL, False)
+    for copy in summing_level:
+        copy.wait_recv()
+    take_z(1, 0)
+    take_z(1, 1)
+    values = absorb_level(
+        tile_of(part),
+        x_high,
+        y_high,
+        [got_x[1, s] for s in range(2)],
+        [[got_xr[1, 2 * s + t : 2 * s + t + 1, :] for t in range(2)] for s in range(2)],
+        z_row,
+        low,
+        high,
+    )
     weight = occupation_ref[0]
     squares = [weight * value * value for value in values]
     for m in range(20):
@@ -551,7 +630,6 @@
     store = pltpu.make_async_copy(nat_f.at[pl.ds(0, 108), :], filtered_ref.at[:, 0, :], out_sem)
     store.start()
 
-    is_end = (z_lo == 0) | (z_lo == ZLO - 1)
     B, W, Q, R1, W1 = 0, 1, 2, 3, 4
 
     @pl.when(is_end)
@@ -646,15 +724,20 @@
                 copy.start()
             return made
 
+        def energy_row(v):
+            cells = jnp.sum((grid_ext[0:392, :] * terms[0:392, :]).reshape(49, 8, 128), axis=0)
+            cells = jnp.sum(jnp.where(lane < 64, cells, 0.0), axis=0, keepdims=True)
+            owned = vec[v, 0:CORE_ROWS, :]
+            return cells + onto_row(screen[...] * owned * owned)
+
         sent = [again]
         made = start_sums(2, vec.at[B], 1.0, screened(B), True)
-        sent += made + hand_on(0, B)
+        red_a = start_reduce(0, [dot_row(B, B), energy_row(B)])
+        sent += made + red_a + hand_on(0, B)
         put(W, finish_sums(2, made))
-
-        red_a = start_reduce(0, [dot_row(B, B), dot_row(B, W)])
+        red_b = second_level(0, red_a)
         made = start_sums(3, vec.at[W], 1.0, screened(W), True)
-        red_b = second_level(0, red_a)
-        sent += made + red_a + red_b + hand_on(1, W)
+        sent += made + red_b + hand_on(1, W)
         put(Q, finish_sums(3, made))
         norm_0, image_0 = scalars(0, red_b, 2)
         alpha_0 = norm_0 / image_0
@@ -662,10 +745,6 @@
         vec[R1] = vec[B] - alpha_0 * vec[W]
         vec[W1] = vec[W] - alpha_0 * vec[Q]
         products(vec.at[W1])
-        energy = jnp.sum((grid_ext[0:392, :] * terms[0:392, :]).reshape(49, 8, 128), axis=0)
-        energy = jnp.sum(jnp.where(lane < 64, energy, 0.0), axis=0, keepdims=True)
-        owned = vec[W1, 0:CORE_ROWS, :]
-        energy = energy + onto_row(screen[...] * owned * owned)
         red_a = start_reduce(
             1,
             [
@@ -674,7 +753,7 @@
                 dot_row(R1, W),
                 dot_row(W1, W1),
                 dot_row(W1, W),
-                energy,
+                energy_row(W1),
                 dot_row(W1, Q),
                 dot_row(W, Q),
             ],
@@ -711,7 +790,7 @@
     def _():
         to_last.wait_send()
 
-    for copy in ghosts + summing:
+    for copy in ghosts + ghosts_level + summing + summing_level:
         copy.wait_send()
     store.wait()
 

time: 81.7 us -> 81.6 us (level)
  no operation moved by 1% of the time
where the time goes in v3:
time: 81.6 us; the launch traced here: 80.5 us
  Pallas kernels  77.1 us (94%)
  local copies, waits for them, and re-layouts  2.09 us (3%)
  between operations  1.29 us (2%)
    pallas_call x1, Pallas kernels, per_device(): pl.pallas_call(kernel, out_shape=(jax.ShapeDtypeStruct((108, 1, 128), F32...  77.1 us
    unnamed x4, local copies, waits for them, and re-layouts  2.09 us

profile of v3, /device:TPU:6, one launch (start us, length us, event | category | flops | bytes accessed | tf_op | source)
XLA Modules:
  0.0 80.5 jit_solution(5179533936703477710)
XLA Ops:
  1.3 77.1 %step.1 = (f32[108,1,128]{2,1,0:T(1,128)}, f32[108,128]{1,0:T(8,128)}) custom-call(f32[108,1,128]{2,1,0:T(1,128)} %bitcast.13, f32[108,1,128]{2,1,0:T(1,128)} %bitcast.14, f32[108,128]{1,0:T(8,128)} %bitcast.10, f32[108,128]{1,0:T(8,128)} %bitcast.11, f32[1]{0:T(128)S(6)} %copy.12.occupation_ref, f32[1,64]{1,0:T(1,128)} %bitcast.15, f32[343,343]{1,0:T(8,128)} %matrix_ref.1, ...), custom_call_target="tpu_custom_call" | custom-call | tf_op jit(solution)/shard_map/step/pallas_call | solution.py:827
  78.4 0.0 copy-start
  78.4 1.5 %copy.13 = f32[1,13824]{1,0:T(1,128)} copy(f32[1,13824]{1,0:T(1,128)} %bitcast.12) | data formatting | bytes 110592
  79.9 0.0 copy-done
  79.9 0.6 copy.14
Async XLA Ops:
  78.4 1.5 %copy-start = (f32[108,128]{1,0:T(8,128)S(1)}, f32[108,128]{1,0:T(8,128)}, u32[]{:S(2)}) copy-start(f32[108,128]{1,0:T(8,128)} %get-tuple-element.5) | copy-start | bytes 165892

commit v4 on v2

--- a/solution.py
+++ b/solution.py
@@ -19,6 +19,24 @@
 TILES = 38
 CORE_ROWS = 288
 ROWS = 8 * TILES
+
+
+class Guarded:
+    def __init__(self, copy, goes, comes):
+        self.copy, self.goes, self.comes = copy, goes, comes
+
+    def start(self):
+        pl.when(self.goes)(self.copy.start)
+
+    def wait_send(self):
+        pl.when(self.goes)(self.copy.wait_send)
+
+    def wait_recv(self):
+        pl.when(self.comes)(self.copy.wait_recv)
+
+
+def back(step):
+    return tuple(-d for d in step)
 
 
 def side(step):
@@ -280,7 +298,7 @@
 def kernel(
     states_ref, previous_ref, potential_ref, screening_ref, occupation_ref, scale_ref, matrix_ref, ids_ref,
     filtered_ref, field_ref,
-    pad, raw_matrix, ids, table, padded_matrix, cell_matrix, scales,
+    pad, raw_matrix, ids, given_scale, occupied, table, padded_matrix, cell_matrix, scales,
     own, screen, vec, grid_ext, terms, part, faces,
     sent_x, sent_y, sent_z, sent_e, got_x, got_y, got_z, got_xr, got_yr, got_e, z_both,
     dens, dens_in, half, half_in, full_in, red_out, red_in, nat, nat_f, factors,
@@ -306,23 +324,53 @@
     def chip(z):
         return (dom, 2 * z + core)
 
-    group_one = [(place(lax.rem(px + e % 4, 4), lax.rem(py + 2 * (e // 4), 4), pz), band) for e in range(1, 8)]
-    group_two = []
+    y_at = lax.div(dom, 8)
+    group_one, group_two = [], []
     for e in range(1, 8):
-        z = lax.rem(pz + e % 4, 4)
-        if e // 4:
-            group_two.append((place(px, py + 1 - 2 * z_hi, z), across))
-        else:
-            group_two.append((place(px, py, z), band))
-
-    greeted = [near(step, False) for step in AROUND]
-    greeted += [near(step, True) for step in AROUND if step[1]]
-    greeted.append(partner)
-    greeted += [chip(lax.rem(z_lo + e, ZLO)) for e in range(1, ZLO)]
-    greeted += group_one + group_two
+        x = lax.rem(px + e % 4, 4)
+        y = py + 1 - 2 * z_hi if e // 4 else py
+        group_one.append((place(x, y, pz), across if e // 4 else band))
+    for e in range(1, 8):
+        group_two.append((lax.rem(dom, 8) + 8 * lax.rem(y_at + e, 8), band))
+
+    is_end = (z_lo == 0) | (z_lo == ZLO - 1)
+    def inside(step):
+        tests = []
+        for at, d in zip((px, py, pz), step):
+            if d:
+                tests.append(at < 3 if d > 0 else at > 0)
+        found = tests[0]
+        for test in tests[1:]:
+            found = found & test
+        return found
+
+    for got in (got_x, got_y, got_z, got_xr, got_yr, got_e):
+        got[...] = jnp.zeros_like(got)
     barrier = pltpu.get_barrier_semaphore()
-    for device in greeted:
+
+    def greet(device):
         pl.semaphore_signal(barrier, inc=1, device_id=device, device_id_type=MESH)
+
+    for step in AROUND:
+        pl.when(inside(step))(lambda step=step: greet(near(step, False)))
+    others = [partner] + [chip(lax.rem(z_lo + e, ZLO)) for e in range(1, ZLO)]
+    for device in others:
+        greet(device)
+
+    @pl.when(is_end)
+    def _():
+        for step in AROUND:
+            if step[1]:
+                pl.when(inside(step))(lambda step=step: greet(near(step, True)))
+        for device in group_one + group_two:
+            greet(device)
+
+    def along(at):
+        return 1 + lax.div(at + 3, 4) + lax.div(6 - at, 4)
+
+    level = along(px) * along(pz)
+    at_end = lax.div(z_lo, ZLO - 1) + lax.div(ZLO - 1 - z_lo, ZLO - 1)
+    n_greeted = level * along(py) - 1 + len(others) + at_end * (level * (along(py) - 1) + len(group_one) + len(group_two))
 
     loads = [
         pltpu.make_async_copy(states_ref.at[:, 0, :], pad.at[0, pl.ds(0, 108), :], in_sem.at[0]),
@@ -331,6 +379,8 @@
         pltpu.make_async_copy(screening_ref, pad.at[3, pl.ds(0, 108), :], in_sem.at[3]),
         pltpu.make_async_copy(matrix_ref, raw_matrix, in_sem.at[4]),
         pltpu.make_async_copy(ids_ref.at[:, pl.ds(0, 128)], ids, in_sem.at[5]),
+        pltpu.make_async_copy(scale_ref, given_scale, in_sem.at[6]),
+        pltpu.make_async_copy(occupation_ref, occupied, in_sem.at[7]),
     ]
     for load in loads:
         load.start()
@@ -384,7 +434,7 @@
         )
 
     def start_copies(at, steps, mirrored):
-        made = [copy_to(at, step, mirrored) for step in steps]
+        made = [Guarded(copy_to(at, step, mirrored), inside(step), inside(back(step))) for step in steps]
         for copy in made:
             copy.start()
         return made
@@ -412,21 +462,28 @@
             grid_ext[8 * v : 8 * v + 8, :] = tiles[v]
         terms[...] = cell_terms(grid_ext[...], cell_matrix[0], cell_matrix[1], scales[0:1, :])
 
-    def start_sums(at, source, factor, extra, mirrored):
+    def cell_sums(source, factor, extra):
         products(source)
         folded, x_high, y_high = local_fold(lambda v: terms[8 * v : 8 * v + 8, :])
         for g in range(36):
             part[8 * g : 8 * g + 8, :] = factor * folded[g] + extra(g)
-        x_high, y_high = factor * x_high, factor * y_high
-        faces[0], faces[1] = x_high, y_high
-        xs, ys, edges = shared(tile_of(part), x_high, y_high)
+        faces[0], faces[1] = factor * x_high, factor * y_high
+
+    def put_level(at, xs, x_high, y_high):
         for s in range(2):
+            k = 6 if s == 0 else 0
             sent_x[at, s] = xs[s]
-            sent_y[at, s] = ys[s]
-            put_z(at, s, part, 6 if s == 0 else 0)
-            k = 6 if s == 0 else 0
+            put_z(at, s, part, k)
             sent_z[at, s, 18:19, :] = x_high[k : k + 1]
             sent_z[at, s, 19:20, :] = y_high[k : k + 1]
+
+    def start_sums(at, source, factor, extra, mirrored):
+        cell_sums(source, factor, extra)
+        x_high, y_high = faces[0], faces[1]
+        xs, ys, edges = shared(tile_of(part), x_high, y_high)
+        put_level(at, xs, x_high, y_high)
+        for s in range(2):
+            sent_y[at, s] = ys[s]
         for c in range(4):
             sent_e[at, c : c + 1, :] = edges[c]
         return start_copies(at, AROUND, mirrored)
@@ -455,7 +512,8 @@
     sent_y[0, 1] = y_tile
     sent_e[0, 3:4, :] = column_to_row(own[0:8, :], 0)
     put_z(0, 1, own, 0)
-    pl.semaphore_wait(barrier, len(greeted))
+
+    pl.semaphore_wait(barrier, n_greeted)
     ghosts = start_copies(0, BELOW, False)
 
     for load in loads[1:]:
@@ -482,7 +540,7 @@
     _, lane_64 = iotas(64)
     first_id = 6 * 49 * ((lane_64 & 63) >> 3) + 6 * (lane_64 & 7)
     matches = jnp.where(first_id == jnp.broadcast_to(ids[:, 0:1], (64, 128)), 1.0, 0.0).astype(F32)
-    given = jnp.broadcast_to(scale_ref[...], (8, 64))
+    given = jnp.broadcast_to(given_scale[...], (8, 64))
     scales[...] = jnp.dot(given, matches, precision=lax.Precision.HIGHEST, preferred_element_type=F32)
 
     for copy in ghosts:
@@ -503,7 +561,7 @@
         vec[1, 8 * m : 8 * m + 8, :] = compact[m]
     summing = start_sums(1, vec.at[1], 0.5 * FILTER_SCALE, tile_of(vec.at[0]), False)
     values = finish_sums(1, summing)
-    weight = occupation_ref[0]
+    weight = occupied[...]
     squares = [weight * value * value for value in values]
     for m in range(20):
         tile = squares[m]
@@ -551,7 +609,6 @@
     store = pltpu.make_async_copy(nat_f.at[pl.ds(0, 108), :], filtered_ref.at[:, 0, :], out_sem)
     store.start()
 
-    is_end = (z_lo == 0) | (z_lo == ZLO - 1)
     B, W, Q, R1, W1 = 0, 1, 2, 3, 4
 
     @pl.when(is_end)
@@ -646,15 +703,20 @@
                 copy.start()
             return made
 
+        def energy_row(v):
+            cells = jnp.sum((grid_ext[0:392, :] * terms[0:392, :]).reshape(49, 8, 128), axis=0)
+            cells = jnp.sum(jnp.where(lane < 64, cells, 0.0), axis=0, keepdims=True)
+            owned = vec[v, 0:CORE_ROWS, :]
+            return cells + onto_row(screen[...] * owned * owned)
+
         sent = [again]
         made = start_sums(2, vec.at[B], 1.0, screened(B), True)
-        sent += made + hand_on(0, B)
+        red_a = start_reduce(0, [dot_row(B, B), energy_row(B)])
+        sent += made + red_a + hand_on(0, B)
         put(W, finish_sums(2, made))
-
-        red_a = start_reduce(0, [dot_row(B, B), dot_row(B, W)])
+        red_b = second_level(0, red_a)
         made = start_sums(3, vec.at[W], 1.0, screened(W), True)
-        red_b = second_level(0, red_a)
-        sent += made + red_a + red_b + hand_on(1, W)
+        sent += made + red_b + hand_on(1, W)
         put(Q, finish_sums(3, made))
         norm_0, image_0 = scalars(0, red_b, 2)
         alpha_0 = norm_0 / image_0
@@ -662,10 +724,6 @@
         vec[R1] = vec[B] - alpha_0 * vec[W]
         vec[W1] = vec[W] - alpha_0 * vec[Q]
         products(vec.at[W1])
-        energy = jnp.sum((grid_ext[0:392, :] * terms[0:392, :]).reshape(49, 8, 128), axis=0)
-        energy = jnp.sum(jnp.where(lane < 64, energy, 0.0), axis=0, keepdims=True)
-        owned = vec[W1, 0:CORE_ROWS, :]
-        energy = energy + onto_row(screen[...] * owned * owned)
         red_a = start_reduce(
             1,
             [
@@ -674,7 +732,7 @@
                 dot_row(R1, W),
                 dot_row(W1, W1),
                 dot_row(W1, W),
-                energy,
+                energy_row(W1),
                 dot_row(W1, Q),
                 dot_row(W, Q),
             ],
@@ -744,16 +802,17 @@
 def per_device(states, previous, potential, screening, occupation, cell_scale, cell_matrix, connectivity):
     vmem = pl.BlockSpec(memory_space=pltpu.VMEM)
     anywhere = pl.BlockSpec(memory_space=pl.ANY)
-    scalar = pl.BlockSpec(memory_space=pltpu.SMEM)
     filtered, field = pl.pallas_call(
         kernel,
         out_shape=(jax.ShapeDtypeStruct((108, 1, 128), F32), jax.ShapeDtypeStruct((108, 128), F32)),
-        in_specs=[anywhere] * 4 + [scalar, vmem, anywhere, anywhere],
+        in_specs=[anywhere] * 8,
         out_specs=(anywhere, vmem),
         scratch_shapes=[
             pltpu.VMEM((4, 144, 128), F32),
             pltpu.VMEM((343, 343), F32),
             pltpu.VMEM((64, 128), jnp.int32),
+            pltpu.VMEM((1, 64), F32),
+            pltpu.VMEM((1, 1), F32),
             pltpu.VMEM((384, 384), BF16),
             pltpu.VMEM((384, 384), F32),
             pltpu.VMEM((2, 400, 512), BF16),
@@ -786,7 +845,7 @@
             pltpu.VMEM((3, 144, 128), F32),
             pltpu.VMEM((144, 128), F32),
             pltpu.VMEM((2, 8, 128), F32),
-            pltpu.SemaphoreType.DMA((6,)),
+            pltpu.SemaphoreType.DMA((8,)),
             pltpu.SemaphoreType.DMA,
             pltpu.SemaphoreType.DMA((4, 26)),
             pltpu.SemaphoreType.DMA((4, 26)),
@@ -802,7 +861,7 @@
         previous.reshape(108, 1, 128),
         potential.reshape(108, 128),
         screening.reshape(108, 128),
-        occupation,
+        occupation.reshape(1, 1),
         cell_scale.reshape(1, 64),
         cell_matrix,
         connectivity.T,

time: 81.7 us -> 76.7 us (0.939)
  the two profiles are of different devices: /device:TPU:6 before, /device:TPU:64 now
where the time goes in v4:
time: 76.7 us; the launch traced here: 76.5 us
  Pallas kernels  73.1 us (95%)
  local copies, waits for them, and re-layouts  2.09 us (3%)
  between operations  1.29 us (2%)
    pallas_call x1, Pallas kernels, per_device(): pl.pallas_call(kernel, out_shape=(jax.ShapeDtypeStruct((108, 1, 128), F32...  73.1 us
    unnamed x4, local copies, waits for them, and re-layouts  2.09 us

profile of v4, /device:TPU:64, one launch (start us, length us, event | category | flops | bytes accessed | tf_op | source)
XLA Modules:
  0.0 76.5 jit_solution(12872179627593851854)
XLA Ops:
  1.3 73.1 %step.1 = (f32[108,1,128]{2,1,0:T(1,128)}, f32[108,128]{1,0:T(8,128)}) custom-call(f32[108,1,128]{2,1,0:T(1,128)} %bitcast.15, f32[108,1,128]{2,1,0:T(1,128)} %bitcast.16, f32[108,128]{1,0:T(8,128)} %bitcast.12, f32[108,128]{1,0:T(8,128)} %bitcast.13, f32[1,1]{1,0:T(1,128)} %bitcast.9.occupation_ref, f32[1,64]{1,0:T(1,128)} %bitcast.17, ...), custom_call_target="tpu_custom_call" | custom-call | tf_op jit(solution)/shard_map/step/pallas_call | solution.py:805
  74.4 0.0 copy-start
  74.4 1.5 %copy.13 = f32[1,13824]{1,0:T(1,128)} copy(f32[1,13824]{1,0:T(1,128)} %bitcast.14) | data formatting | bytes 110592
  75.8 0.0 copy-done
  75.8 0.6 copy.14
Async XLA Ops:
  74.4 1.5 %copy-start = (f32[108,128]{1,0:T(8,128)S(1)}, f32[108,128]{1,0:T(8,128)}, u32[]{:S(2)}) copy-start(f32[108,128]{1,0:T(8,128)} %get-tuple-element.5) | copy-start | bytes 165892

commit v5 on v4

--- a/solution.py
+++ b/solution.py
@@ -301,8 +301,8 @@
     pad, raw_matrix, ids, given_scale, occupied, table, padded_matrix, cell_matrix, scales,
     own, screen, vec, grid_ext, terms, part, faces,
     sent_x, sent_y, sent_z, sent_e, got_x, got_y, got_z, got_xr, got_yr, got_e, z_both,
-    dens, dens_in, half, half_in, full_in, red_out, red_in, nat, nat_f, factors,
-    in_sem, out_sem, halo_send, halo_recv, band_send, band_recv, red_send, red_recv,
+    dens, dens_in, half, half_in, full_in, red_out, red_in, last_out, last_in, nat, nat_f, factors,
+    in_sem, out_sem, halo_send, halo_recv, band_send, band_recv, red_send, red_recv, last_send, last_recv,
 ):
     dom, band = lax.axis_index("dom"), lax.axis_index("band")
     px, py, pz = lax.rem(dom, 4), lax.rem(lax.div(dom, 4), 4), lax.div(dom, 16)
@@ -332,6 +332,12 @@
         group_one.append((place(x, y, pz), across if e // 4 else band))
     for e in range(1, 8):
         group_two.append((lax.rem(dom, 8) + 8 * lax.rem(y_at + e, 8), band))
+
+    served = [
+        [(device, 2 * jnp.where(z_lo == 0, 1 + s, ZLO - 2 - s) + core) for device in [dom] + [d for d, _ in group_two]]
+        for s in range(2)
+    ]
+    serving = 2 * jnp.where(z_lo < ZLO // 2, 0, ZLO - 1) + core
 
     is_end = (z_lo == 0) | (z_lo == ZLO - 1)
     def inside(step):
@@ -362,15 +368,21 @@
         for step in AROUND:
             if step[1]:
                 pl.when(inside(step))(lambda step=step: greet(near(step, True)))
-        for device in group_one + group_two:
+        for device in group_one + group_two + served[0][1:] + served[1][1:]:
             greet(device)
+
+    @pl.when(jnp.logical_not(is_end))
+    def _():
+        for device, _ in group_two:
+            greet((device, serving))
 
     def along(at):
         return 1 + lax.div(at + 3, 4) + lax.div(6 - at, 4)
 
     level = along(px) * along(pz)
     at_end = lax.div(z_lo, ZLO - 1) + lax.div(ZLO - 1 - z_lo, ZLO - 1)
-    n_greeted = level * along(py) - 1 + len(others) + at_end * (level * (along(py) - 1) + len(group_one) + len(group_two))
+    n_greeted = level * along(py) - 1 + len(others) + len(group_two)
+    n_greeted = n_greeted + at_end * (level * (along(py) - 1) + len(group_one) + 2 * len(group_two))
 
     loads = [
         pltpu.make_async_copy(states_ref.at[:, 0, :], pad.at[0, pl.ds(0, 108), :], in_sem.at[0]),
@@ -611,6 +623,23 @@
 
     B, W, Q, R1, W1 = 0, 1, 2, 3, 4
 
+    def last_copy(at_send, e, device):
+        return pltpu.make_async_remote_copy(
+            src_ref=last_out,
+            dst_ref=last_in.at[e],
+            send_sem=last_send.at[at_send],
+            recv_sem=last_recv.at[e],
+            device_id=device,
+            device_id_type=MESH,
+        )
+
+    def write_field(got, known):
+        for e in range(1, 8):
+            got = got + last_in[e]
+        got = jnp.sum(got, axis=1, keepdims=True)
+        c_b, c_w, c_q = combine(*[known[m : m + 1, 0:1] for m in range(3)], *[got[m : m + 1] for m in range(8)])
+        field_ref[...] = c_b * nat[0, 0:108, :] + c_w * nat[1, 0:108, :] + c_q * nat[2, 0:108, :]
+
     @pl.when(is_end)
     def _():
         arrived = [band_copy(half, half_in.at[s], 1, 1 + s, partner) for s in range(ZLO - 1)]
@@ -720,6 +749,8 @@
         put(Q, finish_sums(3, made))
         norm_0, image_0 = scalars(0, red_b, 2)
         alpha_0 = norm_0 / image_0
+        factors[0] = jnp.where(row == 0, wide(alpha_0), jnp.where(row == 1, wide(norm_0), wide(image_0)))
+        sent += onward(factors.at[0], factors.at[1], 3)
 
         vec[R1] = vec[B] - alpha_0 * vec[W]
         vec[W1] = vec[W] - alpha_0 * vec[Q]
@@ -738,13 +769,16 @@
             ],
         )
         sent += hand_on(2, Q)
-        red_b = second_level(1, red_a)
-        norm_1, rw, rv, ww, wv, waw, wav, vav = scalars(1, red_b, 8)
-        c_b, c_w, c_q = combine(alpha_0, norm_0, image_0, norm_1, rw, rv, ww, wv, waw, wav, vav)
-        tile = jnp.where(row == 0, wide(c_b), jnp.where(row == 1, wide(c_w), wide(c_q)))
-        factors[0] = tile
-        sent += red_a + red_b + onward(factors.at[0], factors.at[1], 3)
-        field_ref[...] = c_b * nat[0, 0:108, :] + c_w * nat[1, 0:108, :] + c_q * nat[2, 0:108, :]
+        last_out[...] = take(1, 0, red_a)
+        last = [last_copy(e, e, device) for e, device in enumerate(group_two, 1)]
+        for m in range(2):
+            last += [last_copy(8 * (m + 1) + e, e, device) for e, device in enumerate(served[m])]
+        for copy in last:
+            copy.start()
+        sent += red_a + last
+        for copy in last[:7]:
+            copy.wait_recv()
+        write_field(last_out[...], factors[0])
         for copy in sent:
             copy.wait_send()
 
@@ -753,11 +787,9 @@
         for n in range(3):
             band_copy(nat.at[n, 0:112], nat.at[n, 0:112], 4, 7 + n, partner).wait_recv()
         band_copy(factors.at[0], factors.at[1], 4, 10, partner).wait_recv()
-        field_ref[...] = (
-            factors[1, 0:1, :] * nat[0, 0:108, :]
-            + factors[1, 1:2, :] * nat[1, 0:108, :]
-            + factors[1, 2:3, :] * nat[2, 0:108, :]
-        )
+        for e in range(8):
+            last_copy(e, e, partner).wait_recv()
+        write_field(last_in[0], factors[1])
 
     swap.wait_send()
 
@@ -842,6 +874,8 @@
             pltpu.VMEM((2, 80, 128), F32),
             pltpu.VMEM((2, 2, 8, 128), F32),
             pltpu.VMEM((2, 2, 7, 8, 128), F32),
+            pltpu.VMEM((8, 128), F32),
+            pltpu.VMEM((8, 8, 128), F32),
             pltpu.VMEM((3, 144, 128), F32),
             pltpu.VMEM((144, 128), F32),
             pltpu.VMEM((2, 8, 128), F32),
@@ -853,6 +887,8 @@
             pltpu.SemaphoreType.DMA((11,)),
             pltpu.SemaphoreType.DMA((2, 2, 7)),
             pltpu.SemaphoreType.DMA((2, 2, 7)),
+            pltpu.SemaphoreType.DMA((24,)),
+            pltpu.SemaphoreType.DMA((8,)),
         ],
         compiler_params=pltpu.CompilerParams(collective_id=0, has_side_effects=True),
         name="step",

time: 76.7 us -> 75.6 us (0.986)
  the two profiles are of different devices: /device:TPU:64 before, /device:TPU:6 now
where the time goes in v5:
time: 75.6 us; the launch traced here: 74.3 us
  Pallas kernels  70.9 us (94%)
  local copies, waits for them, and re-layouts  2.09 us (3%)
  between operations  1.29 us (2%)
    pallas_call x1, Pallas kernels, per_device(): pl.pallas_call(kernel, out_shape=(jax.ShapeDtypeStruct((108, 1, 128), F32...  70.9 us
    unnamed x4, local copies, waits for them, and re-layouts  2.09 us

profile of v5, /device:TPU:6, one launch (start us, length us, event | category | flops | bytes accessed | tf_op | source)
XLA Modules:
  0.0 74.3 jit_solution(4624379672388012155)
XLA Ops:
  1.3 70.9 %step.1 = (f32[108,1,128]{2,1,0:T(1,128)}, f32[108,128]{1,0:T(8,128)}) custom-call(f32[108,1,128]{2,1,0:T(1,128)} %bitcast.15, f32[108,1,128]{2,1,0:T(1,128)} %bitcast.16, f32[108,128]{1,0:T(8,128)} %bitcast.12, f32[108,128]{1,0:T(8,128)} %bitcast.13, f32[1,1]{1,0:T(1,128)} %bitcast.9.occupation_ref, f32[1,64]{1,0:T(1,128)} %bitcast.17, ...), custom_call_target="tpu_custom_call" | custom-call | tf_op jit(solution)/shard_map/step/pallas_call | solution.py:837
  72.2 0.0 copy-start
  72.2 1.5 %copy.13 = f32[1,13824]{1,0:T(1,128)} copy(f32[1,13824]{1,0:T(1,128)} %bitcast.14) | data formatting | bytes 110592
  73.7 0.0 copy-done
  73.7 0.6 copy.14
Async XLA Ops:
  72.2 1.5 %copy-start = (f32[108,128]{1,0:T(8,128)S(1)}, f32[108,128]{1,0:T(8,128)}, u32[]{:S(2)}) copy-start(f32[108,128]{1,0:T(8,128)} %get-tuple-element.5) | copy-start | bytes 165892

commit v6 on v5

--- a/solution.py
+++ b/solution.py
@@ -575,14 +575,15 @@
     values = finish_sums(1, summing)
     weight = occupied[...]
     squares = [weight * value * value for value in values]
-    for m in range(20):
-        tile = squares[m]
-        if m + 20 < TILES:
-            tile = tile + roll(squares[m + 20], 64)
+    two_faces = squares[36] + roll(squares[37], 64)
+    for m in range(18):
+        tile = squares[m] + roll(squares[m + 18], 64)
+        if m < 7:
+            tile = jnp.where(row == 7, wide(two_faces[m : m + 1]), tile)
         dens[8 * m : 8 * m + 8, :] = tile
 
-    mine = pl.multiple_of(80 * core, 8)
-    other = pl.multiple_of(80 * (1 - core), 8)
+    mine = pl.multiple_of(72 * core, 8)
+    other = pl.multiple_of(72 * (1 - core), 8)
 
     def band_copy(src, dst, at_send, at_recv, device):
         return pltpu.make_async_remote_copy(
@@ -594,12 +595,12 @@
             device_id_type=MESH,
         )
 
-    swap = band_copy(dens.at[pl.ds(other, 80), :], dens_in, 0, 0, partner)
+    swap = band_copy(dens.at[pl.ds(other, 72), :], dens_in, 0, 0, partner)
     swap.start()
     for m in range(36):
         vec[0, 8 * m : 8 * m + 8, :] = values[m]
     swap.wait_recv()
-    half[...] = dens[pl.ds(mine, 80), :] + dens_in[...]
+    half[...] = dens[pl.ds(mine, 72), :] + dens_in[...]
 
     not_first, not_last = z_lo > 0, z_lo < ZLO - 1
     slot_first = jnp.maximum(z_lo - 1, 0)
@@ -618,7 +619,7 @@
     natural = from_cells([jnp.where(row < 6, vec[0, 8 * g : 8 * g + 8, :], 0.0) for g in range(36)], table[...])
     for c in range(18):
         nat_f[pl.ds(c, 8, stride=18), :] = natural[c]
-    store = pltpu.make_async_copy(nat_f.at[pl.ds(0, 108), :], filtered_ref.at[:, 0, :], out_sem)
+    store = pltpu.make_async_copy(nat_f.at[pl.ds(0, 108), :], filtered_ref, out_sem)
     store.start()
 
     B, W, Q, R1, W1 = 0, 1, 2, 3, 4
@@ -656,11 +657,16 @@
             jnp.where(core == 0, full_in[0], full_in[1]),
             jnp.where(core == 0, full_in[1], full_in[0]),
         )
-        for m in range(20):
-            tile = both[m // 10][8 * (m % 10) : 8 * (m % 10) + 8]
+        two_faces = jnp.zeros((8, 128), F32)
+        for m in range(18):
+            tile = both[m // 9][8 * (m % 9) : 8 * (m % 9) + 8]
+            if m < 7:
+                two_faces = jnp.where(row == m, wide(tile[7:8]), two_faces)
+            tile = jnp.where(row < 7, tile, 0.0)
             vec[B, 8 * m : 8 * m + 8, :] = jnp.where(lane < 64, tile, 0.0)
-            if m + 20 < TILES:
-                vec[B, 8 * (m + 20) : 8 * (m + 20) + 8, :] = jnp.where(lane < 64, roll(tile, 64), 0.0)
+            vec[B, 8 * (m + 18) : 8 * (m + 18) + 8, :] = jnp.where(lane < 64, roll(tile, 64), 0.0)
+        vec[B, 288:296, :] = jnp.where(lane < 64, two_faces, 0.0)
+        vec[B, 296:304, :] = jnp.where(lane < 64, roll(two_faces, 64), 0.0)
 
         def put(v, tiles):
             for m in range(TILES):
@@ -836,7 +842,7 @@
     anywhere = pl.BlockSpec(memory_space=pl.ANY)
     filtered, field = pl.pallas_call(
         kernel,
-        out_shape=(jax.ShapeDtypeStruct((108, 1, 128), F32), jax.ShapeDtypeStruct((108, 128), F32)),
+        out_shape=(jax.ShapeDtypeStruct((108, 128), F32), jax.ShapeDtypeStruct((108, 128), F32)),
         in_specs=[anywhere] * 8,
         out_specs=(anywhere, vmem),
         scratch_shapes=[
@@ -867,11 +873,11 @@
             pltpu.VMEM((4, 8, 128), F32),
             pltpu.VMEM((4, 3, 8, 128), F32),
             pltpu.VMEM((2, 2, 24, 128), F32),
-            pltpu.VMEM((160, 128), F32),
-            pltpu.VMEM((80, 128), F32),
-            pltpu.VMEM((80, 128), F32),
-            pltpu.VMEM((5, 80, 128), F32),
-            pltpu.VMEM((2, 80, 128), F32),
+            pltpu.VMEM((144, 128), F32),
+            pltpu.VMEM((72, 128), F32),
+            pltpu.VMEM((72, 128), F32),
+            pltpu.VMEM((5, 72, 128), F32),
+            pltpu.VMEM((2, 72, 128), F32),
             pltpu.VMEM((2, 2, 8, 128), F32),
             pltpu.VMEM((2, 2, 7, 8, 128), F32),
             pltpu.VMEM((8, 128), F32),
@@ -902,7 +908,8 @@
         cell_matrix,
         connectivity.T,
     )
-    return filtered.reshape(1, 13824), field.reshape(13824)
+    flat = lax.optimization_barrier(filtered.reshape(13824))
+    return flat.reshape(1, 13824), field.reshape(13824)
 
 
 def solution(mesh):

time: 75.6 us -> 75.4 us (level)
    reshape x0 -> x1, local copies, waits for them, and re-layouts: none -> 1.5 us  [per_device(): return (flat.reshape(1, 13824), field.reshape(13824))]
    unnamed x4 -> x3, local copies, waits for them, and re-layouts: 2.09 us -> 0.63 us
where the time goes in v6:
time: 75.4 us; the launch traced here: 74.2 us
  Pallas kernels  70.8 us (94%)
  local copies, waits for them, and re-layouts  2.13 us (3%)
  between operations  1.29 us (2%)
    pallas_call x1, Pallas kernels, per_device(): pl.pallas_call(kernel, out_shape=(jax.ShapeDtypeStruct((108, 128), F32),...  70.8 us

profile of v6, /device:TPU:6, one launch (start us, length us, event | category | flops | bytes accessed | tf_op | source)
XLA Modules:
  0.0 74.2 jit_solution(8321494971298796965)
XLA Ops:
  1.3 70.8 %step.1 = (f32[108,128]{1,0:T(8,128)}, f32[108,128]{1,0:T(8,128)}) custom-call(f32[108,1,128]{2,1,0:T(1,128)} %bitcast.15, f32[108,1,128]{2,1,0:T(1,128)} %bitcast.16, f32[108,128]{1,0:T(8,128)} %bitcast.13, f32[108,128]{1,0:T(8,128)} %bitcast.14, f32[1,1]{1,0:T(1,128)} %bitcast.9.occupation_ref, f32[1,64]{1,0:T(1,128)} %bitcast.17, f32[343,343]{1,0:T(8,128)} %matrix_ref.1, ...), custom_call_target="tpu_custom_call" | custom-call | tf_op jit(solution)/shard_map/step/pallas_call | solution.py:843
  72.1 0.0 copy-start
  72.1 1.5 %reshape.38 = f32[1,13824]{1,0:T(1,128)} reshape(f32[13824]{0:T(1024)} %bitcast.12) | data formatting | bytes 110592 | tf_op jit(solution)/shard_map/reshape | solution.py:912
  73.6 0.0 copy-done
  73.6 0.6 copy.12
Async XLA Ops:
  72.1 1.5 %copy-start = (f32[108,128]{1,0:T(8,128)S(1)}, f32[108,128]{1,0:T(8,128)}, u32[]{:S(2)}) copy-start(f32[108,128]{1,0:T(8,128)} %get-tuple-element.5) | copy-start | bytes 165892

commit v7 on v6

--- a/solution.py
+++ b/solution.py
@@ -474,8 +474,9 @@
             grid_ext[8 * v : 8 * v + 8, :] = tiles[v]
         terms[...] = cell_terms(grid_ext[...], cell_matrix[0], cell_matrix[1], scales[0:1, :])
 
-    def cell_sums(source, factor, extra):
+    def cell_sums(source, factor, extra, first):
         products(source)
+        first()
         folded, x_high, y_high = local_fold(lambda v: terms[8 * v : 8 * v + 8, :])
         for g in range(36):
             part[8 * g : 8 * g + 8, :] = factor * folded[g] + extra(g)
@@ -489,8 +490,8 @@
             sent_z[at, s, 18:19, :] = x_high[k : k + 1]
             sent_z[at, s, 19:20, :] = y_high[k : k + 1]
 
-    def start_sums(at, source, factor, extra, mirrored):
-        cell_sums(source, factor, extra)
+    def start_sums(at, source, factor, extra, mirrored, first=lambda: None):
+        cell_sums(source, factor, extra, first)
         x_high, y_high = faces[0], faces[1]
         xs, ys, edges = shared(tile_of(part), x_high, y_high)
         put_level(at, xs, x_high, y_high)
@@ -619,7 +620,7 @@
     natural = from_cells([jnp.where(row < 6, vec[0, 8 * g : 8 * g + 8, :], 0.0) for g in range(36)], table[...])
     for c in range(18):
         nat_f[pl.ds(c, 8, stride=18), :] = natural[c]
-    store = pltpu.make_async_copy(nat_f.at[pl.ds(0, 108), :], filtered_ref, out_sem)
+    store = pltpu.make_async_copy(nat_f.at[pl.ds(0, 108), :], filtered_ref.at[:, 0, :], out_sem)
     store.start()
 
     B, W, Q, R1, W1 = 0, 1, 2, 3, 4
@@ -745,11 +746,18 @@
             return cells + onto_row(screen[...] * owned * owned)
 
         sent = [again]
-        made = start_sums(2, vec.at[B], 1.0, screened(B), True)
-        red_a = start_reduce(0, [dot_row(B, B), energy_row(B)])
+        red_a = []
+        made = start_sums(
+            2,
+            vec.at[B],
+            1.0,
+            screened(B),
+            True,
+            lambda: red_a.extend(start_reduce(0, [dot_row(B, B), energy_row(B)])),
+        )
         sent += made + red_a + hand_on(0, B)
+        red_b = second_level(0, red_a)
         put(W, finish_sums(2, made))
-        red_b = second_level(0, red_a)
         made = start_sums(3, vec.at[W], 1.0, screened(W), True)
         sent += made + red_b + hand_on(1, W)
         put(Q, finish_sums(3, made))
@@ -837,12 +845,25 @@
     return wv + alpha_0 * vav
 
 
+def pass_on(filtered_in, field_in, filtered_out, field_out, filtered_here, field_here, sem):
+    pairs = ((field_in, field_here, field_out), (filtered_in, filtered_here, filtered_out))
+    taken = [pltpu.make_async_copy(a, b, sem.at[m]) for m, (a, b, _) in enumerate(pairs)]
+    given = [pltpu.make_async_copy(b, c, sem.at[2 + m]) for m, (_, b, c) in enumerate(pairs)]
+    for copy in taken:
+        copy.start()
+    for one, two in zip(taken, given):
+        one.wait()
+        two.start()
+    for copy in given:
+        copy.wait()
+
+
 def per_device(states, previous, potential, screening, occupation, cell_scale, cell_matrix, connectivity):
     vmem = pl.BlockSpec(memory_space=pltpu.VMEM)
     anywhere = pl.BlockSpec(memory_space=pl.ANY)
     filtered, field = pl.pallas_call(
         kernel,
-        out_shape=(jax.ShapeDtypeStruct((108, 128), F32), jax.ShapeDtypeStruct((108, 128), F32)),
+        out_shape=(jax.ShapeDtypeStruct((108, 1, 128), F32), jax.ShapeDtypeStruct((108, 128), F32)),
         in_specs=[anywhere] * 8,
         out_specs=(anywhere, vmem),
         scratch_shapes=[
@@ -908,8 +929,19 @@
         cell_matrix,
         connectivity.T,
     )
-    flat = lax.optimization_barrier(filtered.reshape(13824))
-    return flat.reshape(1, 13824), field.reshape(13824)
+    filtered, field = pl.pallas_call(
+        pass_on,
+        out_shape=(jax.ShapeDtypeStruct((108, 1, 128), F32), jax.ShapeDtypeStruct((108, 128), F32)),
+        in_specs=[anywhere] * 2,
+        out_specs=(anywhere, anywhere),
+        scratch_shapes=[
+            pltpu.VMEM((108, 1, 128), F32),
+            pltpu.VMEM((108, 128), F32),
+            pltpu.SemaphoreType.DMA((4,)),
+        ],
+        name="pass_on",
+    )(filtered, field)
+    return filtered.reshape(1, 13824), field.reshape(13824)
 
 
 def solution(mesh):

time: 75.4 us -> 74.8 us (level)
  local copies, waits for them, and re-layouts: 2.13 us -> 0 us
  Pallas kernels: 70.8 us -> 72.3 us
    pallas_call x1 -> x2, Pallas kernels: 70.8 us -> 72.3 us  [the longest x1 70.8 us: per_device(): pl.pallas_call(kernel, out_shape=(jax.ShapeDtypeStruct((108, 1, 128), F32...]
    reshape x1 -> x0, local copies, waits for them, and re-layouts: 1.5 us -> none  [per_device(): return (flat.reshape(1, 13824), field.reshape(13824))]
where the time goes in v7:
time: 74.8 us; the launch traced here: 73.6 us
  Pallas kernels  72.3 us (97%)
  between operations  1.29 us (2%)
    pallas_call x1, Pallas kernels, per_device(): pl.pallas_call(kernel, out_shape=(jax.ShapeDtypeStruct((108, 1, 128), F32...  70.8 us
    pallas_call x1, Pallas kernels, per_device(): pl.pallas_call(pass_on, out_shape=(jax.ShapeDtypeStruct((108, 1, 128), F3...  1.5 us

profile of v7, /device:TPU:6, one launch (start us, length us, event | category | flops | bytes accessed | tf_op | source)
XLA Modules:
  0.0 73.6 jit_solution(16390302777708961354)
XLA Ops:
  1.3 70.8 %step.1 = (f32[108,1,128]{2,1,0:T(1,128)}, f32[108,128]{1,0:T(8,128)}) custom-call(f32[108,1,128]{2,1,0:T(1,128)} %bitcast.13, f32[108,1,128]{2,1,0:T(1,128)} %bitcast.14, f32[108,128]{1,0:T(8,128)} %bitcast.11, f32[108,128]{1,0:T(8,128)} %bitcast.12, f32[1,1]{1,0:T(1,128)} %bitcast.9.occupation_ref, f32[1,64]{1,0:T(1,128)} %bitcast.15, ...), custom_call_target="tpu_custom_call" | custom-call | tf_op jit(solution)/shard_map/step/pallas_call | solution.py:864
  72.1 1.5 %pass_on.1 = (f32[108,1,128]{2,1,0:T(1,128)}, f32[108,128]{1,0:T(8,128)}) custom-call(f32[108,1,128]{2,1,0:T(1,128)} %get-tuple-element.6.filtered_in, f32[108,128]{1,0:T(8,128)} %get-tuple-element.7.field_in), custom_call_target="tpu_custom_call" | custom-call | tf_op jit(solution)/shard_map/pass_on/pallas_call | solution.py:932

commit v8 on v7

--- a/solution.py
+++ b/solution.py
@@ -845,27 +845,14 @@
     return wv + alpha_0 * vav
 
 
-def pass_on(filtered_in, field_in, filtered_out, field_out, filtered_here, field_here, sem):
-    pairs = ((field_in, field_here, field_out), (filtered_in, filtered_here, filtered_out))
-    taken = [pltpu.make_async_copy(a, b, sem.at[m]) for m, (a, b, _) in enumerate(pairs)]
-    given = [pltpu.make_async_copy(b, c, sem.at[2 + m]) for m, (_, b, c) in enumerate(pairs)]
-    for copy in taken:
-        copy.start()
-    for one, two in zip(taken, given):
-        one.wait()
-        two.start()
-    for copy in given:
-        copy.wait()
-
-
 def per_device(states, previous, potential, screening, occupation, cell_scale, cell_matrix, connectivity):
     vmem = pl.BlockSpec(memory_space=pltpu.VMEM)
     anywhere = pl.BlockSpec(memory_space=pl.ANY)
     filtered, field = pl.pallas_call(
         kernel,
-        out_shape=(jax.ShapeDtypeStruct((108, 1, 128), F32), jax.ShapeDtypeStruct((108, 128), F32)),
+        out_shape=(pltpu.VMEM((108, 1, 128), F32), pltpu.VMEM((108, 128), F32)),
         in_specs=[anywhere] * 8,
-        out_specs=(anywhere, vmem),
+        out_specs=(vmem, vmem),
         scratch_shapes=[
             pltpu.VMEM((4, 144, 128), F32),
             pltpu.VMEM((343, 343), F32),
@@ -929,18 +916,6 @@
         cell_matrix,
         connectivity.T,
     )
-    filtered, field = pl.pallas_call(
-        pass_on,
-        out_shape=(jax.ShapeDtypeStruct((108, 1, 128), F32), jax.ShapeDtypeStruct((108, 128), F32)),
-        in_specs=[anywhere] * 2,
-        out_specs=(anywhere, anywhere),
-        scratch_shapes=[
-            pltpu.VMEM((108, 1, 128), F32),
-            pltpu.VMEM((108, 128), F32),
-            pltpu.SemaphoreType.DMA((4,)),
-        ],
-        name="pass_on",
-    )(filtered, field)
     return filtered.reshape(1, 13824), field.reshape(13824)
 
 

time: 74.8 us -> 73.9 us (0.988)
  Pallas kernels: 72.3 us -> 70.2 us
  local copies, waits for them, and re-layouts: 0 us -> 1.25 us
    pallas_call x2 -> x1, Pallas kernels: 72.3 us -> 70.2 us  [per_device(): pl.pallas_call(kernel, out_shape=(pltpu.VMEM((108, 1, 128), F32), pltpu.V...]
    unnamed x0 -> x2, local copies, waits for them, and re-layouts: none -> 1.25 us
where the time goes in v8:
time: 73.9 us; the launch traced here: 72.7 us
  Pallas kernels  70.2 us (95%)
  between operations  1.29 us (2%)
  local copies, waits for them, and re-layouts  1.25 us (2%)
    pallas_call x1, Pallas kernels, per_device(): pl.pallas_call(kernel, out_shape=(pltpu.VMEM((108, 1, 128), F32), pltpu.V...  70.2 us

profile of v8, /device:TPU:6, one launch (start us, length us, event | category | flops | bytes accessed | tf_op | source)
XLA Modules:
  0.0 72.7 jit_solution(12321993755618043366)
XLA Ops:
  1.3 70.2 %step.1 = (f32[108,1,128]{2,1,0:T(1,128)S(1)}, f32[108,128]{1,0:T(8,128)S(1)}) custom-call(f32[108,1,128]{2,1,0:T(1,128)} %bitcast.15, f32[108,1,128]{2,1,0:T(1,128)} %bitcast.16, f32[108,128]{1,0:T(8,128)} %bitcast.13, f32[108,128]{1,0:T(8,128)} %bitcast.14, f32[1,1]{1,0:T(1,128)} %bitcast.9.occupation_ref, f32[1,64]{1,0:T(1,128)} %bitcast.17, ...), custom_call_target="tpu_custom_call" | custom-call | tf_op jit(solution)/shard_map/step/pallas_call | solution.py:851
  71.5 0.6 copy.12
  72.1 0.6 copy.13
